TPU v7x, 256 devices: a whole 4x4x8 slice. The times are simulated.
256 devices in a mesh: date: 32 (over z, x), rng: 8 (over y, core).
Axes of the slice: x: 4, y: 4, z: 8, core: 2. Of those that a mesh axis runs over, the one named last changes fastest.
Arguments:
- slc: bfloat16 [256, 2, 256, 4096], P('date', None, None, 'rng')
- offsets: int32 [256, 32, 2], P('date', 'rng'), may hold values from -2 to 2, as said below
- taps: float32 [256, 8], P('date'), may hold values from 0.05 to 1
- pairs: int32 [1024, 2], replicated, may hold values from 0 to 255, as said below
Outputs:
- series: float32 [2, 256, 64, 256], P(None, None, 'date', 'rng')
Inputs may be any that keep to these rules, and one draw needn't show every extreme that they name: `offsets`: every value from -2 to 2 occurs. Every date is the reference of exactly 4 pairs; the secondary date is the reference plus 1 to min(16, 255), counted modulo 256.
All inputs are finite; a program needn't handle non-finite values.
Results may differ from a plain program's by a relative error of at most 0.0018.
Values may be sent and summed in bfloat16 or wider, within the bound.
No kernel may reach another device: no remote copies, remote signals or barrier semaphores. Data moves between devices by JAX's collectives and lax.ppermute only.
A program may use at most 256 MiB of HBM per device.

v0:
```python
import functools

import jax
import jax.numpy as jnp
from jax import lax
from jax.experimental import pallas as pl
from jax.experimental.pallas import tpu as pltpu
from jax.sharding import Mesh
from jax.sharding import PartitionSpec as P


TAPS = 8
EPS = 1e-06
REG = 0.1
DATES = 256
PAIRS = 1024
UNIT = 8
WINDOW = 48
REFS = 32
INNER = (8, 24)
SLOTS = 4
NEWTON = 9
UNROLL = 4
STEP = 4
CHUNKS = ((1, 2), (0, 3))

F32 = jnp.float32
BF16 = jnp.bfloat16


def iota(shape, dim):
    return lax.broadcasted_iota(jnp.int32, shape, dim)


def dot(a, b, precision=None):
    return jnp.dot(a, b, precision=precision, preferred_element_type=F32)


def split(v):
    high = v.astype(BF16)
    return high, (v - high.astype(F32)).astype(BF16)


def resample_kernel(tiles, needed, halo_in, pack, off_ref, taps_ref, *refs):
    refs = list(refs)
    data = {t: refs.pop(0) for t in needed}
    halo = {t: refs.pop(0) for t in halo_in}
    out = refs.pop(0)
    packs = [refs.pop(0) for _ in range(2)] if pack else None
    perm = refs.pop(0)
    i = pl.program_id(0)

    @pl.when(i == 0)
    def _():
        o = iota((256, 256), 0)
        row = 32 * (o & 7) + 8 * (o >> 6) + 4 * ((o >> 3) & 1) + ((o >> 4) & 3)
        gap = row - iota((256, 256), 1)
        for s in range(5):
            perm[s] = jnp.where(gap == s - 2, 1.0, 0.0).astype(BF16)
        if pack:
            for ref in packs:
                ref[...] = jnp.zeros_like(ref)

    j, l = iota((128, 128), 0), iota((128, 128), 1)
    near = jnp.abs(j - l) < 64
    lane = iota((8, 128), 1)
    at = iota((256, 128), 1)
    if pack:
        j4, l4 = iota((128 * STEP, 128), 0), iota((128 * STEP, 128), 1)
        slot, j4 = 8 * (i * STEP + (j4 >> 7)), j4 & 127
        left = jnp.where((j4 < 8) & (l4 == slot + j4), 1.0, 0.0).astype(BF16)
        right = jnp.where((j4 >= 120) & (l4 == slot + j4 - 104), 1.0, 0.0).astype(BF16)
        for c in range(2):
            for ref, src, sel in ((packs[0], data[0], left), (packs[1], data[3], right)):
                side = jnp.concatenate([src[e, c] for e in range(STEP)], axis=1)
                ref[c] += dot(side, sel).astype(BF16)
    for e in range(STEP):
        d = i * STEP + e
        for n, t in enumerate(tiles):
            row_shift = off_ref[t, 0, d]
            k = (off_ref[t, 1, d] + 3 - lane) & 127
            base = jnp.zeros((8, 128), F32)
            for tap in range(TAPS):
                base = jnp.where(k == tap, taps_ref[d, tap], base)
            ring = pltpu.roll(jnp.concatenate([base] * 16, axis=0), 0, 1, stride=1, stride_axis=0)
            high = ring.astype(BF16).astype(F32)
            rows = []
            for part in (high, ring - high):
                own = jnp.where(near, part, 0.0)
                far = part - own
                if t == 0:
                    edge = jnp.concatenate([far[120:128]] * 16, axis=0)
                    far = jnp.where(j < 16, far, jnp.where((j >> 3) == 2 + d, edge, 0.0))
                elif t == 3:
                    edge = jnp.concatenate([far[0:8]] * 16, axis=0)
                    far = jnp.where(j >= 112, far, jnp.where((j >> 3) == d, edge, 0.0))
                rows.append(jnp.concatenate([own.astype(BF16), far.astype(BF16)], axis=0))
            weights = jnp.concatenate(rows, axis=1)
            parts = []
            for c in range(2):
                cur = data[t][e, c]
                if t == 0:
                    mixed = jnp.where(at < 16, data[1][e, c], halo[0][c])
                elif t == 3:
                    mixed = jnp.where(at < 112, halo[3][c], data[2][e, c])
                else:
                    mixed = jnp.where(at < 64, data[t + 1][e, c], data[t - 1][e, c])
                lhs = jnp.concatenate([cur, mixed], axis=1)
                wide = dot(lhs, weights)
                parts.append((wide[:, :128] + wide[:, 128:]).astype(BF16))
            both = jnp.concatenate(parts, axis=1)
            moved = dot(perm[row_shift + 2], both).astype(BF16)
            for g in range(4):
                for c in range(2):
                    out[g, n, e, c] = moved[64 * g : 64 * g + 64, 128 * c : 128 * c + 128]


def resample(tiles, slc, halos, offs, taps, pack):
    needed = {s for t in tiles for s in (t - 1, t, t + 1) if 0 <= s < 4}
    needed = sorted(needed | {0, 3} if pack else needed)
    halo_in = [t for t in tiles if t in (0, 3)]
    count = len(tiles)
    whole = pl.BlockSpec((2, 256, 128), lambda d, *_: (0, 0, 0))
    in_specs = [
        pl.BlockSpec((STEP, 2, 256, 128), functools.partial(lambda t, d, *_: (d, 0, 0, t), t))
        for t in needed
    ] + [whole] * len(halo_in)
    out_specs = [pl.BlockSpec((4, count, STEP, 2, 64, 128), lambda d, *_: (0, 0, d, 0, 0, 0))]
    out_shape = [jax.ShapeDtypeStruct((4, count, UNIT, 2, 64, 128), BF16)]
    if pack:
        out_specs += [whole] * 2
        out_shape += [jax.ShapeDtypeStruct((2, 256, 128), BF16)] * 2
    return pl.pallas_call(
        functools.partial(resample_kernel, tiles, needed, halo_in, pack),
        out_shape=out_shape,
        grid_spec=pltpu.PrefetchScalarGridSpec(
            num_scalar_prefetch=2,
            grid=(UNIT // STEP,),
            in_specs=in_specs,
            out_specs=out_specs,
            scratch_shapes=[pltpu.VMEM((5, 256, 256), BF16)],
        ),
    )(offs, taps, *([slc] * len(needed)), *[halos[t] for t in halo_in])


def table_kernel(first_ref, pairs_ref, out_ref):
    a, b = pairs_ref[0:1, :], pairs_ref[1:2, :]
    date = (iota((REFS, PAIRS), 0) + first_ref[0]) & (DATES - 1)
    key = jnp.where(a == date, iota((REFS, PAIRS), 1) * DATES + b, 1 << 20)
    lane = iota((REFS, 128), 1)
    w = iota((REFS, 128), 0)
    out = jnp.zeros((REFS, 128), jnp.int32)
    for s in range(SLOTS):
        low = jnp.min(key, axis=1, keepdims=True)
        key = jnp.where(key == low, 1 << 20, key)
        away = ((low & (DATES - 1)) - w - first_ref[0]) & (DATES - 1)
        out = jnp.where(lane == s, w + away, out)
    out_ref[...] = out


def table(first, pairs_t):
    return pl.pallas_call(
        table_kernel,
        out_shape=jax.ShapeDtypeStruct((REFS, 128), jnp.int32),
        grid_spec=pltpu.PrefetchScalarGridSpec(
            num_scalar_prefetch=1,
            grid=(1,),
            in_specs=[pl.BlockSpec((2, PAIRS), lambda i, *_: (0, 0))],
            out_specs=pl.BlockSpec((REFS, 128), lambda i, *_: (0, 0)),
        ),
        name="table",
    )(first, pairs_t)


def inverse_kernel(pairs_ref, out_ref):
    date = iota((DATES, PAIRS), 0)
    one = jnp.where(pairs_ref[0:1, :] == date, 1.0, 0.0)
    design = (one - jnp.where(pairs_ref[1:2, :] == date, 1.0, 0.0)).astype(BF16)
    graph = lax.dot_general(
        design, design, (((1,), (1,)), ((), ())), preferred_element_type=F32
    )
    eye = jnp.where(iota((DATES, DATES), 0) == iota((DATES, DATES), 1), 1.0, 0.0)
    top = 2.0 * jnp.max(graph, keepdims=True) + REG
    rho = (top - REG) / (top + REG)
    start = 2.0 / (top + REG)
    square = rho * rho
    beta = 2.0 / (2.0 - square)
    rho = square / (2.0 - square)
    x = (beta * start) * (2.0 * eye - start * (graph + REG * eye))
    whole = graph.astype(BF16)

    def step(_, carry):
        x, rho = carry
        square = rho * rho
        beta = 2.0 / (2.0 - square)
        high, mid = split(x)
        low = (x - high.astype(F32) - mid.astype(F32)).astype(BF16)
        gap = eye - REG * x - (dot(whole, low) + dot(whole, mid) + dot(whole, high))
        gap_h, gap_l = split(gap)
        more = dot(high, gap_l) + dot(mid, gap_h) + dot(high, gap_h)
        return beta * (x + more), square / (2.0 - square)

    out_ref[...] = lax.fori_loop(0, NEWTON, step, (x, rho))[0]


def inverse(pairs_t):
    return pl.pallas_call(
        inverse_kernel,
        out_shape=jax.ShapeDtypeStruct((DATES, DATES), F32),
        name="inverse",
    )(pairs_t)


HALF = 16
RAW = HALF * SLOTS * 8


def fold(v):
    return v[0:16] + v[16:32] + v[32:48] + v[48:64]


def copies_of(sources, win, sem, count):
    return [
        [
            pltpu.make_async_copy(src.at[n], win.at[n, pl.ds(UNIT * u, UNIT)], sem.at[n, u])
            for u, src in sources
        ]
        for n in range(count)
    ]


def look_sums(tiles, copies, tab_ref, place, dates, win, sums, squares, raw, power, before):
    for group in copies:
        for copy in group:
            copy.start()
    k, l = iota((512, 128), 0), iota((512, 128), 1)
    kp, lp = iota((256, 128), 0), iota((256, 128), 1)
    for n, t in enumerate(tiles):
        sel = jnp.where(l == 32 * (k >> 7) + 8 * t + ((k & 127) >> 4), 1.0, 0.0).astype(BF16)
        selp = jnp.where(
            (lp & 63) == 32 * (kp >> 7) + 8 * t + ((kp & 127) >> 4), 1.0, 0.0
        ).astype(BF16)
        for copy in copies[n]:
            copy.wait()
        row = 0
        for start, stop in dates:

            def power_step(i, _):
                tops = []
                for e in range(4):
                    v = win[n, start + 4 * i + e].astype(F32)
                    tops.append(fold(v[0] * v[0] + v[1] * v[1]))
                at = pl.ds(pl.multiple_of(row + i * 32, 32), 32)
                for h in range(2):
                    v = jnp.concatenate([v[8 * h : 8 * h + 8] for v in tops], axis=0)
                    for m, half in enumerate(split(v)):
                        squares[m, at, 128 * h : 128 * h + 128] = half
                return 0

            lax.fori_loop(0, (stop - start) // 4, power_step, 0, unroll=2)
            row += 8 * (stop - start)
        total = dot(squares[0], selp) + dot(squares[1], selp)
        if n > 0:
            total = total + power[...]
        elif before:
            total = total + before[1][...]
        power[...] = total

        def pair_step(i, _):
            w = place(i)
            a = win[n, w].astype(F32)
            for half in range(2):
                got = []
                for s in (2 * half, 2 * half + 1):
                    b = win[n, tab_ref[w, s]].astype(F32)
                    re = fold(a[0] * b[0] + a[1] * b[1])
                    im = fold(a[1] * b[0] - a[0] * b[1])
                    got.append((re[0:8], re[8:16], im[0:8], im[8:16]))
                at = pl.ds(pl.multiple_of(i * 32 + 16 * half, 16), 16)
                for g in range(4):
                    v = jnp.concatenate([got[0][g], got[1][g]], axis=0)
                    for m, part in enumerate(split(v)):
                        sums[m, at, 128 * g : 128 * g + 128] = part
            return 0

        lax.fori_loop(0, HALF, pair_step, 0, unroll=UNROLL)
        looks = dot(sums[0], sel) + dot(sums[1], sel)
        if n > 0:
            looks = looks + raw[...]
        elif before:
            looks = looks + before[0][...]
        raw[...] = looks


def scale_and_scatter(tab_ref, place, raw, whole, rhs):
    for s in range(SLOTS):
        rhs[s] = jnp.zeros_like(rhs[s])

    def scale_step(i, _):
        w = place(i)
        pa = whole[pl.ds(pl.multiple_of(w * 8, 8), 8), :]
        total = jnp.zeros((8, 128), F32)
        for s in range(SLOTS):
            pb = whole[pl.ds(pl.multiple_of(tab_ref[w, s] * 8, 8), 8), :]
            at = pl.multiple_of(i * 32 + 8 * s, 8)
            v = raw[pl.ds(at, 8), :] * lax.rsqrt(pa * pb + EPS)
            total = total + v
            raw[pl.ds(at, 8), :] = v
        rhs[SLOTS, pl.ds(pl.multiple_of(w * 8, 8), 8), :] += total
        return 0

    lax.fori_loop(0, HALF, scale_step, 0, unroll=4)

    def scatter_step(i, _):
        for s in range(SLOTS):
            at = pl.multiple_of(tab_ref[place(i), s] * 8, 8)
            rhs[s, pl.ds(at, 8), :] -= raw[pl.ds(pl.multiple_of(i * 32 + 8 * s, 8), 8), :]
        return 0

    lax.fori_loop(0, HALF, scatter_step, 0, unroll=4)
    rhs[SLOTS] = (rhs[0] + rhs[1]) + (rhs[2] + rhs[3]) + rhs[SLOTS]


def inner_kernel(tiles, first, last, tab_ref, mine, *refs):
    refs = list(refs)
    before = () if first else (refs.pop(0), refs.pop(0))
    if last:
        rhs_out, power, win, sums, squares, sem, raw, whole, rhs = refs
    else:
        raw, power, win, sums, squares, sem = refs
    copies = copies_of([(u + 1, mine.at[u]) for u in range(4)], win, sem, len(tiles))

    def place(i):
        return i + INNER[0]

    look_sums(
        tiles, copies, tab_ref, place, ((8, 40),), win, sums, squares, raw, power, before
    )
    if last:
        whole[64:320] = power[...]
        rhs[SLOTS] = jnp.zeros_like(rhs[SLOTS])
        scale_and_scatter(tab_ref, place, raw, whole, rhs)
        rhs_out[...] = rhs[SLOTS]


def outer_kernel(tiles, first, last, tab_ref, below, mine, above, *refs):
    refs = list(refs)
    before = () if first else (refs.pop(0), refs.pop(0))
    if last:
        inner_rhs, inner_power = refs.pop(0), refs.pop(0)
        out_ref, win, sums, squares, sem, raw, power, whole, rhs = refs
    else:
        raw, power, win, sums, squares, sem = refs
    sources = [(u + 1, mine.at[u]) for u in range(4)] + [(0, below), (5, above)]
    copies = copies_of(sources, win, sem, len(tiles))

    def place(i):
        return jnp.where(i < INNER[0], i, i + INNER[1] - INNER[0])

    look_sums(
        tiles,
        copies,
        tab_ref,
        place,
        ((0, 8), (40, 48)),
        win,
        sums,
        squares,
        raw,
        power,
        before,
    )
    if last:
        whole[0:64] = power[0:64]
        whole[64:320] = inner_power[...]
        whole[320:384] = power[64:128]
        rhs[SLOTS] = inner_rhs[...]
        scale_and_scatter(tab_ref, place, raw, whole, rhs)
        for z in range(8):
            out_ref[z] = rhs[SLOTS, pl.ds(z, WINDOW, stride=8), :]


def coherence(inner, tiles, tab, units, before, extra, last):
    count = len(tiles)
    rows = 256 if inner else 128
    vmem = pl.BlockSpec(memory_space=pltpu.VMEM)
    raw = jax.ShapeDtypeStruct((RAW, 128), F32)
    power = jax.ShapeDtypeStruct((rows, 128), F32)
    scratch = [
        pltpu.VMEM((count, WINDOW, 2, 64, 128), BF16),
        pltpu.VMEM((2, RAW, 512), BF16),
        pltpu.VMEM((2, rows, 256), BF16),
        pltpu.SemaphoreType.DMA((count, 6)),
    ]
    outs = [raw, power]
    if last:
        scratch.append(pltpu.VMEM((RAW, 128), F32))
        if inner:
            outs = [jax.ShapeDtypeStruct((WINDOW * 8, 128), F32), power]
        else:
            outs = jax.ShapeDtypeStruct((8, WINDOW, 128), F32)
            scratch.append(pltpu.VMEM((rows, 128), F32))
        scratch += [
            pltpu.VMEM((WINDOW * 8, 128), F32),
            pltpu.VMEM((SLOTS + 1, WINDOW * 8, 128), F32),
        ]
    return pl.pallas_call(
        functools.partial(inner_kernel if inner else outer_kernel, tiles, not before, last),
        out_shape=outs,
        in_specs=[pl.BlockSpec(memory_space=pltpu.SMEM)]
        + [pl.BlockSpec(memory_space=pl.ANY)] * len(units)
        + [vmem] * len((*before, *extra)),
        out_specs=[vmem] * 2 if isinstance(outs, list) else vmem,
        scratch_shapes=scratch,
    )(tab, *units, *before, *extra)


def solve_kernel(inv_ref, got_ref, out_ref, rhs):
    for z in range(8):
        early = got_ref[z, 0:16, :] + got_ref[(z + 7) % 8, 32:48, :]
        rhs[32 * z : 32 * z + 16, :] = early
        rhs[32 * z + 16 : 32 * z + 32, :] = got_ref[z, 16:32, :]
        if z == 0:
            rhs[DATES : DATES + 8, :] = early[0:8]
    out_ref[...] = lax.dot_general(
        rhs[8 : DATES + 8, :],
        inv_ref[...],
        (((0,), (0,)), ((), ())),
        precision=lax.Precision.HIGHEST,
        preferred_element_type=F32,
    )


def solve(inv, got):
    return pl.pallas_call(
        solve_kernel,
        out_shape=jax.ShapeDtypeStruct((128, DATES), F32),
        in_specs=[pl.BlockSpec(memory_space=pltpu.VMEM)] * 2,
        out_specs=pl.BlockSpec(memory_space=pltpu.VMEM),
        scratch_shapes=[pltpu.VMEM((DATES + 8, 128), F32)],
        name="solve",
    )(inv, got)


def per_device(slc, offsets, taps, pairs):
    pairs_t = pairs.T
    offs = jnp.transpose(offsets, (1, 2, 0))
    halos = {}
    units = []
    up = [(z, (z + 1) % 8) for z in range(8)]
    down = [(j, i) for i, j in up]
    for n, tiles in enumerate(CHUNKS):
        got = resample(tiles, slc, halos, offs, taps, n == 0)
        if n == 0:
            size = lax.axis_size("rng")
            halos[3] = lax.ppermute(got[1], "rng", [(i + 1, i) for i in range(size - 1)])
            halos[0] = lax.ppermute(got[2], "rng", [(i, i + 1) for i in range(size - 1)])
        mine = lax.all_to_all(got[0], "x", split_axis=0, concat_axis=0, tiled=True)
        below = lax.ppermute(mine[3], "z", up)
        above = lax.ppermute(mine[0], "z", down)
        units.append((below, mine, above))
    first = lax.axis_index("z").astype(jnp.int32) * 32 - 8
    tab = table(first.reshape(1), pairs_t)
    inv = inverse(pairs_t)
    ins, outs = (), ()
    for n, tiles in enumerate(CHUNKS):
        last = n == len(CHUNKS) - 1
        ins = coherence(True, tiles, tab, units[n][1:2], ins, (), last)
        outs = coherence(False, tiles, tab, units[n], outs, ins if last else (), last)
    got = lax.all_to_all(outs, "z", split_axis=0, concat_axis=0, tiled=True)
    series = solve(inv, got)
    return jnp.transpose(series.reshape(2, 2, 32, DATES), (0, 3, 1, 2))


def solution(mesh):
    fine = Mesh(mesh.devices.reshape(8, 4, 8), ("z", "x", "rng"))
    date = ("z", "x")
    return jax.shard_map(
        per_device,
        mesh=fine,
        in_specs=(P(date, None, None, "rng"), P(date, "rng", None), P(date, None), P()),
        out_specs=P(None, None, date, "rng"),
        check_vma=False,
    )
```

profile of v0, /device:TPU:16, one launch (start us, length us, event | category | flops | bytes accessed | tf_op | source)
XLA Modules:
  0.0 128.5 jit_solution(10749270844228728189)
XLA Ops:
  0.0 8.9 %shard_map.46 = (bf16[4,2,8,2,64,128]{5,4,3,2,1,0:T(8,128)(2,1)}, bf16[2,256,128]{2,1,0:T(8,128)(2,1)}, bf16[2,256,128]{2,1,0:T(8,128)(2,1)}) custom-call(s32[4,2,8]{2,1,0:T(2,128)} %bitcast.16, f32[8,8]{1,0:T(8,128)} %taps_ref.3, bf16[8,2,256,512]{3,2,1,0:T(8,128)(2,1)} %refs_3_.3, bf16[8,2,256,512]{3,2,1,0:T(8,128)(2,1)} %refs_3_.3, ...), custom_call_target="tpu_custom_call" | custom-call | tf_op jit(solution)/shard_map/pallas_call | solution.py:133
  8.9 4.4 %all-to-all-start.1 = ((bf16[4,2,8,2,64,128]{5,4,3,2,1,0:T(8,128)(2,1)}), bf16[4,2,8,2,64,128]{5,4,3,2,1,0:T(8,128)(2,1)S(1)}, u32[]{:S(2)}, u32[]{:S(2)}) async-start(bf16[4,2,8,2,64,128]{5,4,3,2,1,0:T(8,128)(2,1)} %get-tuple-element.16), calls=%async_computation.1 | async-start | bytes 4194304 | tf_op jit(solution)/shard_map/all_to_all | solution.py:458
  13.3 1.9 %collective-permute-start = (bf16[2,256,128]{2,1,0:T(8,128)(2,1)S(1)}, bf16[2,256,128]{2,1,0:T(8,128)(2,1)S(1)}, u32[]{:S(2)}, u32[]{:S(2)}) collective-permute-start(bf16[2,256,128]{2,1,0:T(8,128)(2,1)S(1)} %copy-done.9), channel_id=1, source_target_pairs={{0,1},{1,2},{2,3},{3,4},{4,5},{5,6},{6,7},{8,9},{9,10},{10,11},{11... | collective-permute-start | bytes 393224 | tf_op jit(solution)/shard_map/ppermute | solution.py:457
  15.3 3.6 %collective-permute-start.1 = (bf16[2,256,128]{2,1,0:T(8,128)(2,1)S(1)}, bf16[2,256,128]{2,1,0:T(8,128)(2,1)S(1)}, u32[]{:S(2)}, u32[]{:S(2)}) collective-permute-start(bf16[2,256,128]{2,1,0:T(8,128)(2,1)S(1)} %copy-done.8), channel_id=1, source_target_pairs={{1,0},{2,1},{3,2},{4,3},{5,4},{6,5},{7,6},{9,8},{10,9},{11,10},{12... | collective-permute-start | bytes 393224 | tf_op jit(solution)/shard_map/ppermute | solution.py:456
  19.6 1.8 %collective-permute-done.1.refs_5_ = bf16[2,256,128]{2,1,0:T(8,128)(2,1)S(1)} collective-permute-done((bf16[2,256,128]{2,1,0:T(8,128)(2,1)S(1)}, bf16[2,256,128]{2,1,0:T(8,128)(2,1)S(1)}, u32[]{:S(2)}, u32[]{:S(2)}) %collective-permute-start.1) | collective-permute-done | bytes 131104 | tf_op jit(solution)/shard_map/ppermute | solution.py:456
  22.0 8.8 %shard_map.47 = bf16[4,2,8,2,64,128]{5,4,3,2,1,0:T(8,128)(2,1)} custom-call(s32[4,2,8]{2,1,0:T(2,128)} %bitcast.17, f32[8,8]{1,0:T(8,128)} %taps_ref.3, bf16[8,2,256,512]{3,2,1,0:T(8,128)(2,1)} %refs_3_.3, bf16[8,2,256,512]{3,2,1,0:T(8,128)(2,1)} %refs_3_.3, bf16[8,2,256,512]{3,2,1,0:T(8,128)(2,1)} %refs_3_.3, bf16[8,2,256,512]{3,2,1,0:T(8,128)(2,1)} %refs_3_.3, ...), custom_call_target="tpu_custom_call" | custom-call | tf_op jit(solution)/shard_map/pallas_call | solution.py:133
  30.8 8.8 %all-to-all-done.1.mine = bf16[4,2,8,2,64,128]{5,4,3,2,1,0:T(8,128)(2,1)S(1)} async-done(((bf16[4,2,8,2,64,128]{5,4,3,2,1,0:T(8,128)(2,1)}), bf16[4,2,8,2,64,128]{5,4,3,2,1,0:T(8,128)(2,1)S(1)}, u32[]{:S(2)}, u32[]{:S(2)}) %all-to-all-start.1) | async-done | bytes 2097184 | tf_op jit(solution)/shard_map/all_to_all | solution.py:458
  39.7 4.5 %all-to-all-start = ((bf16[4,2,8,2,64,128]{5,4,3,2,1,0:T(8,128)(2,1)}), bf16[4,2,8,2,64,128]{5,4,3,2,1,0:T(8,128)(2,1)}, u32[]{:S(2)}, u32[]{:S(2)}) async-start(bf16[4,2,8,2,64,128]{5,4,3,2,1,0:T(8,128)(2,1)} %shard_map.47), calls=%async_computation | async-start | bytes 4194304 | tf_op jit(solution)/shard_map/all_to_all | solution.py:458
  44.3 5.9 %collective-permute-start.5 = (bf16[2,8,2,64,128]{4,3,2,1,0:T(8,128)(2,1)S(1)}, bf16[2,8,2,64,128]{4,3,2,1,0:T(8,128)(2,1)S(1)}, u32[]{:S(2)}, u32[]{:S(2)}) collective-permute-start(bf16[2,8,2,64,128]{4,3,2,1,0:T(8,128)(2,1)S(1)} %get-tuple-element.23), channel_id=1, source_target_pairs={{32,0},{64,32},{96,64},{128,96},{160,128},{192,160},{224,192},{0,2... | collective-permute-start | bytes 1572872 | tf_op jit(solution)/shard_map/ppermute | solution.py:460
  50.2 19.5 %all-to-all-done.mine = bf16[4,2,8,2,64,128]{5,4,3,2,1,0:T(8,128)(2,1)} async-done(((bf16[4,2,8,2,64,128]{5,4,3,2,1,0:T(8,128)(2,1)}), bf16[4,2,8,2,64,128]{5,4,3,2,1,0:T(8,128)(2,1)}, u32[]{:S(2)}, u32[]{:S(2)}) %all-to-all-start) | async-done | bytes 2097184 | tf_op jit(solution)/shard_map/all_to_all | solution.py:458
  69.7 2.3 %slice_bitcast_fusion.2 = (bf16[2,8,2,64,128]{4,3,2,1,0:T(8,128)(2,1)}, bf16[2,8,2,64,128]{4,3,2,1,0:T(8,128)(2,1)}) fusion(bf16[4,2,8,2,64,128]{5,4,3,2,1,0:T(8,128)(2,1)} %all-to-all-done.mine), kind=kLoop, calls=%fused_computation.2 | loop fusion | bytes 2097152 | tf_op jit(solution)/shard_map/squeeze | solution.py:460
  72.0 5.9 %collective-permute-start.3 = (bf16[2,8,2,64,128]{4,3,2,1,0:T(8,128)(2,1)}, bf16[2,8,2,64,128]{4,3,2,1,0:T(8,128)(2,1)S(1)}, u32[]{:S(2)}, u32[]{:S(2)}) collective-permute-start(bf16[2,8,2,64,128]{4,3,2,1,0:T(8,128)(2,1)} %get-tuple-element.25), channel_id=1, source_target_pairs={{32,0},{64,32},{96,64},{128,96},{160,128},{192,160},{224,192},{0,2... | collective-permute-start | bytes 1572872 | tf_op jit(solution)/shard_map/ppermute | solution.py:460
  77.8 2.0 %table.1.tab_ref = s32[32,128]{1,0:T(8,128)} custom-call(s32[1]{0:T(128)} %bitcast.1.first_ref, s32[2,1024]{1,0:T(2,128)} %bitcast.14), custom_call_target="tpu_custom_call" | custom-call | tf_op jit(solution)/shard_map/table/pallas_call | solution.py:162
  79.8 7.1 %shard_map.49 = (f32[512,128]{1,0:T(8,128)}, f32[256,128]{1,0:T(8,128)}) custom-call(s32[32,128]{1,0:T(8,128)} %table.1.tab_ref, bf16[4,2,8,2,64,128]{5,4,3,2,1,0:T(8,128)(2,1)} %copy-done), custom_call_target="tpu_custom_call" | custom-call | tf_op jit(solution)/shard_map/pallas_call | solution.py:407
  86.9 7.5 %shard_map.50 = (f32[384,128]{1,0:T(8,128)}, f32[256,128]{1,0:T(8,128)}) custom-call(s32[32,128]{1,0:T(8,128)} %table.1.tab_ref, bf16[4,2,8,2,64,128]{5,4,3,2,1,0:T(8,128)(2,1)} %all-to-all-done.mine, f32[512,128]{1,0:T(8,128)} %get-tuple-element.19.refs_0_, f32[256,128]{1,0:T(8,128)} %get-tuple-element.20.refs_1_), custom_call_target="tpu_custom_call" | custom-call | tf_op jit(solution)/shard_map/pallas_call | solution.py:407
  94.5 0.8 copy-done.4
  95.3 0.8 copy-done.5
  96.1 6.9 %shard_map.48 = (f32[512,128]{1,0:T(8,128)}, f32[128,128]{1,0:T(8,128)}) custom-call(s32[32,128]{1,0:T(8,128)} %table.1.tab_ref, bf16[2,8,2,64,128]{4,3,2,1,0:T(8,128)(2,1)} %copy-done.5, bf16[4,2,8,2,64,128]{5,4,3,2,1,0:T(8,128)(2,1)} %copy-done, bf16[2,8,2,64,128]{4,3,2,1,0:T(8,128)(2,1)} %copy-done.4), custom_call_target="tpu_custom_call" | custom-call | tf_op jit(solution)/shard_map/pallas_call | solution.py:407
  103.0 0.8 copy-done.2
  104.0 7.5 %shard_map.51 = f32[8,48,128]{2,1,0:T(8,128)} custom-call(s32[32,128]{1,0:T(8,128)} %table.1.tab_ref, bf16[2,8,2,64,128]{4,3,2,1,0:T(8,128)(2,1)} %copy-done.3, bf16[4,2,8,2,64,128]{5,4,3,2,1,0:T(8,128)(2,1)} %all-to-all-done.mine, bf16[2,8,2,64,128]{4,3,2,1,0:T(8,128)(2,1)} %copy-done.2, f32[512,128]{1,0:T(8,128)} %get-tuple-element.17.refs_0_, ...), custom_call_target="tpu_custom_call" | custom-call | tf_op jit(solution)/shard_map/pallas_call | solution.py:407
  111.4 4.6 %all-to-all-start.2 = ((f32[8,48,128]{2,1,0:T(8,128)}), f32[8,48,128]{2,1,0:T(8,128)S(1)}, u32[]{:S(2)}, u32[]{:S(2)}) async-start(f32[8,48,128]{2,1,0:T(8,128)} %shard_map.51), calls=%async_computation.2 | async-start | bytes 393216 | tf_op jit(solution)/shard_map/all_to_all | solution.py:470
  116.1 8.4 %inverse.1.inv_ref = f32[256,256]{1,0:T(8,128)} custom-call(s32[2,1024]{1,0:T(2,128)} %bitcast.15), custom_call_target="tpu_custom_call" | custom-call | tf_op jit(solution)/shard_map/inverse/pallas_call | solution.py:207
  124.4 1.4 %all-to-all-done.2.got_ref = f32[8,48,128]{2,1,0:T(8,128)S(1)} async-done(((f32[8,48,128]{2,1,0:T(8,128)}), f32[8,48,128]{2,1,0:T(8,128)S(1)}, u32[]{:S(2)}, u32[]{:S(2)}) %all-to-all-start.2) | async-done | bytes 196640 | tf_op jit(solution)/shard_map/all_to_all | solution.py:470
  126.5 2.0 %solve.1 = f32[128,256]{1,0:T(8,128)} custom-call(f32[256,256]{1,0:T(8,128)} %inverse.1.inv_ref, f32[8,48,128]{2,1,0:T(8,128)} %copy-done.1), custom_call_target="tpu_custom_call" | custom-call | tf_op jit(solution)/shard_map/solve/pallas_call | solution.py:435
  (25 shorter events, 2.3 us)
Async XLA Ops:
  8.9 4.5 %copy-start.9 = (bf16[2,256,128]{2,1,0:T(8,128)(2,1)S(1)}, bf16[2,256,128]{2,1,0:T(8,128)(2,1)}, u32[]{:S(2)}) copy-start(bf16[2,256,128]{2,1,0:T(8,128)(2,1)} %get-tuple-element.14) | copy-start | bytes 393220
  8.9 6.4 %copy-start.8 = (bf16[2,256,128]{2,1,0:T(8,128)(2,1)S(1)}, bf16[2,256,128]{2,1,0:T(8,128)(2,1)}, u32[]{:S(2)}) copy-start(bf16[2,256,128]{2,1,0:T(8,128)(2,1)} %get-tuple-element.15) | copy-start | bytes 393220
  8.9 30.8 %all-to-all-start.1 = ((bf16[4,2,8,2,64,128]{5,4,3,2,1,0:T(8,128)(2,1)}), bf16[4,2,8,2,64,128]{5,4,3,2,1,0:T(8,128)(2,1)S(1)}, u32[]{:S(2)}, u32[]{:S(2)}) async-start(bf16[4,2,8,2,64,128]{5,4,3,2,1,0:T(8,128)(2,1)} %get-tuple-element.16), calls=%async_computation.1 | async-start | bytes 4194304 | tf_op jit(solution)/shard_map/all_to_all | solution.py:458
  13.3 6.3 %collective-permute-start = (bf16[2,256,128]{2,1,0:T(8,128)(2,1)S(1)}, bf16[2,256,128]{2,1,0:T(8,128)(2,1)S(1)}, u32[]{:S(2)}, u32[]{:S(2)}) collective-permute-start(bf16[2,256,128]{2,1,0:T(8,128)(2,1)S(1)} %copy-done.9), channel_id=1, source_target_pairs={{0,1},{1,2},{2,3},{3,4},{4,5},{5,6},{6,7},{8,9},{9,10},{10,11},{11... | collective-permute-start | bytes 393224 | tf_op jit(solution)/shard_map/ppermute | solution.py:457
  15.3 6.1 %collective-permute-start.1 = (bf16[2,256,128]{2,1,0:T(8,128)(2,1)S(1)}, bf16[2,256,128]{2,1,0:T(8,128)(2,1)S(1)}, u32[]{:S(2)}, u32[]{:S(2)}) collective-permute-start(bf16[2,256,128]{2,1,0:T(8,128)(2,1)S(1)} %copy-done.8), channel_id=1, source_target_pairs={{1,0},{2,1},{3,2},{4,3},{5,4},{6,5},{7,6},{9,8},{10,9},{11,10},{12... | collective-permute-start | bytes 393224 | tf_op jit(solution)/shard_map/ppermute | solution.py:456
  19.6 1.8 %copy-start.6 = (bf16[2,256,128]{2,1,0:T(8,128)(2,1)}, bf16[2,256,128]{2,1,0:T(8,128)(2,1)S(1)}, u32[]{:S(2)}) copy-start(bf16[2,256,128]{2,1,0:T(8,128)(2,1)S(1)} %collective-permute-done.refs_4_) | copy-start | bytes 393220
  21.4 0.6 copy-start.7
  39.7 4.5 %copy-start = (bf16[4,2,8,2,64,128]{5,4,3,2,1,0:T(8,128)(2,1)}, bf16[4,2,8,2,64,128]{5,4,3,2,1,0:T(8,128)(2,1)S(1)}, u32[]{:S(2)}) copy-start(bf16[4,2,8,2,64,128]{5,4,3,2,1,0:T(8,128)(2,1)S(1)} %all-to-all-done.1.mine) | copy-start | bytes 6291460
  39.7 30.0 %all-to-all-start = ((bf16[4,2,8,2,64,128]{5,4,3,2,1,0:T(8,128)(2,1)}), bf16[4,2,8,2,64,128]{5,4,3,2,1,0:T(8,128)(2,1)}, u32[]{:S(2)}, u32[]{:S(2)}) async-start(bf16[4,2,8,2,64,128]{5,4,3,2,1,0:T(8,128)(2,1)} %shard_map.47), calls=%async_computation | async-start | bytes 4194304 | tf_op jit(solution)/shard_map/all_to_all | solution.py:458
  44.3 50.2 %collective-permute-start.5 = (bf16[2,8,2,64,128]{4,3,2,1,0:T(8,128)(2,1)S(1)}, bf16[2,8,2,64,128]{4,3,2,1,0:T(8,128)(2,1)S(1)}, u32[]{:S(2)}, u32[]{:S(2)}) collective-permute-start(bf16[2,8,2,64,128]{4,3,2,1,0:T(8,128)(2,1)S(1)} %get-tuple-element.23), channel_id=1, source_target_pairs={{32,0},{64,32},{96,64},{128,96},{160,128},{192,160},{224,192},{0,2... | collective-permute-start | bytes 1572872 | tf_op jit(solution)/shard_map/ppermute | solution.py:460
  50.2 44.3 %collective-permute-start.4 = (bf16[2,8,2,64,128]{4,3,2,1,0:T(8,128)(2,1)S(1)}, bf16[2,8,2,64,128]{4,3,2,1,0:T(8,128)(2,1)S(1)}, u32[]{:S(2)}, u32[]{:S(2)}) collective-permute-start(bf16[2,8,2,64,128]{4,3,2,1,0:T(8,128)(2,1)S(1)} %get-tuple-element.24), channel_id=1, source_target_pairs={{0,32},{32,64},{64,96},{96,128},{128,160},{160,192},{192,224},{224... | collective-permute-start | bytes 1572872 | tf_op jit(solution)/shard_map/ppermute | solution.py:459
  72.0 31.0 %collective-permute-start.3 = (bf16[2,8,2,64,128]{4,3,2,1,0:T(8,128)(2,1)}, bf16[2,8,2,64,128]{4,3,2,1,0:T(8,128)(2,1)S(1)}, u32[]{:S(2)}, u32[]{:S(2)}) collective-permute-start(bf16[2,8,2,64,128]{4,3,2,1,0:T(8,128)(2,1)} %get-tuple-element.25), channel_id=1, source_target_pairs={{32,0},{64,32},{96,64},{128,96},{160,128},{192,160},{224,192},{0,2... | collective-permute-start | bytes 1572872 | tf_op jit(solution)/shard_map/ppermute | solution.py:460
  77.8 25.1 %collective-permute-start.2 = (bf16[2,8,2,64,128]{4,3,2,1,0:T(8,128)(2,1)}, bf16[2,8,2,64,128]{4,3,2,1,0:T(8,128)(2,1)S(1)}, u32[]{:S(2)}, u32[]{:S(2)}) collective-permute-start(bf16[2,8,2,64,128]{4,3,2,1,0:T(8,128)(2,1)} %get-tuple-element.26), channel_id=1, source_target_pairs={{0,32},{32,64},{64,96},{96,128},{128,160},{160,192},{192,224},{224... | collective-permute-start | bytes 1572872 | tf_op jit(solution)/shard_map/ppermute | solution.py:459
  94.5 0.8 copy-start.4
  95.3 0.8 copy-start.5
  103.0 0.8 copy-start.2
  103.0 1.0 copy-start.3
  111.4 14.4 %all-to-all-start.2 = ((f32[8,48,128]{2,1,0:T(8,128)}), f32[8,48,128]{2,1,0:T(8,128)S(1)}, u32[]{:S(2)}, u32[]{:S(2)}) async-start(f32[8,48,128]{2,1,0:T(8,128)} %shard_map.51), calls=%async_computation.2 | async-start | bytes 393216 | tf_op jit(solution)/shard_map/all_to_all | solution.py:470
  125.8 0.7 copy-start.1
where the time goes:
time: 129 us; the launch traced here: 128 us
  Pallas kernels  58.9 us (46%)
  waiting for transfers between devices  32.2 us (25%)
  starting transfers between devices  30.9 us (24%)
  local copies, waits for them, and re-layouts  6.29 us (5%)
    pallas_call x4, Pallas kernels, coherence(): pl.pallas_call(functools.partial(inner_kernel if inner else outer_kernel,...  29 us
    all_to_all x2, waiting for transfers between devices, per_device(): mine = lax.all_to_all(got[0], 'x', split_axis=0, concat_axis=0, tiled=True)  28.3 us
    pallas_call x2, Pallas kernels, resample(): pl.pallas_call(functools.partial(resample_kernel, tiles, needed, halo_in,...  17.6 us
    ppermute x2, starting transfers between devices, per_device(): above = lax.ppermute(mine[0], 'z', down)  11.8 us
    all_to_all x2, starting transfers between devices, per_device(): mine = lax.all_to_all(got[0], 'x', split_axis=0, concat_axis=0, tiled=True)  8.9 us
    pallas_call x1, Pallas kernels, inverse(): pl.pallas_call(inverse_kernel, out_shape=jax.ShapeDtypeStruct((DATES, DAT...  8.38 us
    all_to_all x1, starting transfers between devices, per_device(): got = lax.all_to_all(outs, 'z', split_axis=0, concat_axis=0, tiled=True)  4.63 us
    unnamed x20, local copies, waits for them, and re-layouts  3.87 us
  transfers between devices with their start and end apart: 9, of which 5 were waited for; matrix products, arithmetic and copies ran while one was open for 2% of the time, Pallas kernels for 32%

commit v1 on v0

--- a/solution.py
+++ b/solution.py
@@ -2,6 +2,7 @@
 
 import jax
 import jax.numpy as jnp
+import numpy as np
 from jax import lax
 from jax.experimental import pallas as pl
 from jax.experimental.pallas import tpu as pltpu
@@ -41,28 +42,30 @@
     return high, (v - high.astype(F32)).astype(BF16)
 
 
+def row_moves():
+    o = np.arange(256)[:, None]
+    row = 32 * (o & 7) + 8 * (o >> 6) + 4 * ((o >> 3) & 1) + ((o >> 4) & 3)
+    shift = np.arange(-2, 3)[:, None, None]
+    return (row - shift == np.arange(256)).astype(np.float32)
+
+
 def resample_kernel(tiles, needed, halo_in, pack, off_ref, taps_ref, *refs):
     refs = list(refs)
     data = {t: refs.pop(0) for t in needed}
     halo = {t: refs.pop(0) for t in halo_in}
+    perm = refs.pop(0)
     out = refs.pop(0)
     packs = [refs.pop(0) for _ in range(2)] if pack else None
-    perm = refs.pop(0)
     i = pl.program_id(0)
-
-    @pl.when(i == 0)
-    def _():
-        o = iota((256, 256), 0)
-        row = 32 * (o & 7) + 8 * (o >> 6) + 4 * ((o >> 3) & 1) + ((o >> 4) & 3)
-        gap = row - iota((256, 256), 1)
-        for s in range(5):
-            perm[s] = jnp.where(gap == s - 2, 1.0, 0.0).astype(BF16)
-        if pack:
+    if pack:
+
+        @pl.when(i == 0)
+        def _():
             for ref in packs:
                 ref[...] = jnp.zeros_like(ref)
 
     j, l = iota((128, 128), 0), iota((128, 128), 1)
-    near = jnp.abs(j - l) < 64
+    near = jnp.where(jnp.abs(j - l) < 64, 1.0, 0.0).astype(BF16)
     lane = iota((8, 128), 1)
     at = iota((256, 128), 1)
     if pack:
@@ -83,18 +86,17 @@
             for tap in range(TAPS):
                 base = jnp.where(k == tap, taps_ref[d, tap], base)
             ring = pltpu.roll(jnp.concatenate([base] * 16, axis=0), 0, 1, stride=1, stride_axis=0)
-            high = ring.astype(BF16).astype(F32)
             rows = []
-            for part in (high, ring - high):
-                own = jnp.where(near, part, 0.0)
+            for part in split(ring):
+                own = part * near
                 far = part - own
-                if t == 0:
-                    edge = jnp.concatenate([far[120:128]] * 16, axis=0)
-                    far = jnp.where(j < 16, far, jnp.where((j >> 3) == 2 + d, edge, 0.0))
-                elif t == 3:
-                    edge = jnp.concatenate([far[0:8]] * 16, axis=0)
-                    far = jnp.where(j >= 112, far, jnp.where((j >> 3) == d, edge, 0.0))
-                rows.append(jnp.concatenate([own.astype(BF16), far.astype(BF16)], axis=0))
+                if t in (0, 3):
+                    far = far.astype(F32)
+                    edge = jnp.concatenate([far[120:128] if t == 0 else far[0:8]] * 16, axis=0)
+                    keep = j < 16 if t == 0 else j >= 112
+                    slot = 2 + d if t == 0 else d
+                    far = jnp.where(keep, far, jnp.where((j >> 3) == slot, edge, 0.0)).astype(BF16)
+                rows.append(jnp.concatenate([own, far], axis=0))
             weights = jnp.concatenate(rows, axis=1)
             parts = []
             for c in range(2):
@@ -124,7 +126,8 @@
     in_specs = [
         pl.BlockSpec((STEP, 2, 256, 128), functools.partial(lambda t, d, *_: (d, 0, 0, t), t))
         for t in needed
-    ] + [whole] * len(halo_in)
+    ] + [pl.BlockSpec(memory_space=pltpu.VMEM)] * len(halo_in)
+    in_specs.append(pl.BlockSpec((5, 256, 256), lambda d, *_: (0, 0, 0)))
     out_specs = [pl.BlockSpec((4, count, STEP, 2, 64, 128), lambda d, *_: (0, 0, d, 0, 0, 0))]
     out_shape = [jax.ShapeDtypeStruct((4, count, UNIT, 2, 64, 128), BF16)]
     if pack:
@@ -138,9 +141,8 @@
             grid=(UNIT // STEP,),
             in_specs=in_specs,
             out_specs=out_specs,
-            scratch_shapes=[pltpu.VMEM((5, 256, 256), BF16)],
         ),
-    )(offs, taps, *([slc] * len(needed)), *[halos[t] for t in halo_in])
+    )(offs, taps, *([slc] * len(needed)), *[halos[t] for t in halo_in], jnp.asarray(row_moves(), BF16))
 
 
 def table_kernel(first_ref, pairs_ref, out_ref):
@@ -279,12 +281,11 @@
                 at = pl.ds(pl.multiple_of(i * 32 + 16 * half, 16), 16)
                 for g in range(4):
                     v = jnp.concatenate([got[0][g], got[1][g]], axis=0)
-                    for m, part in enumerate(split(v)):
-                        sums[m, at, 128 * g : 128 * g + 128] = part
+                    sums[at, 128 * g : 128 * g + 128] = v.astype(BF16)
             return 0
 
         lax.fori_loop(0, HALF, pair_step, 0, unroll=UNROLL)
-        looks = dot(sums[0], sel) + dot(sums[1], sel)
+        looks = dot(sums[...], sel)
         if n > 0:
             looks = looks + raw[...]
         elif before:
@@ -388,7 +389,7 @@
     power = jax.ShapeDtypeStruct((rows, 128), F32)
     scratch = [
         pltpu.VMEM((count, WINDOW, 2, 64, 128), BF16),
-        pltpu.VMEM((2, RAW, 512), BF16),
+        pltpu.VMEM((RAW, 512), BF16),
         pltpu.VMEM((2, rows, 256), BF16),
         pltpu.SemaphoreType.DMA((count, 6)),
     ]
@@ -408,7 +409,7 @@
         functools.partial(inner_kernel if inner else outer_kernel, tiles, not before, last),
         out_shape=outs,
         in_specs=[pl.BlockSpec(memory_space=pltpu.SMEM)]
-        + [pl.BlockSpec(memory_space=pl.ANY)] * len(units)
+        + [vmem if len(units) == 3 and u != 1 else pl.BlockSpec(memory_space=pl.ANY) for u in range(len(units))]
         + [vmem] * len((*before, *extra)),
         out_specs=[vmem] * 2 if isinstance(outs, list) else vmem,
         scratch_shapes=scratch,
@@ -442,6 +443,10 @@
     )(inv, got)
 
 
+def near_by(v):
+    return pltpu.with_memory_space_constraint(v, pltpu.VMEM)
+
+
 def per_device(slc, offsets, taps, pairs):
     pairs_t = pairs.T
     offs = jnp.transpose(offsets, (1, 2, 0))
@@ -453,11 +458,11 @@
         got = resample(tiles, slc, halos, offs, taps, n == 0)
         if n == 0:
             size = lax.axis_size("rng")
-            halos[3] = lax.ppermute(got[1], "rng", [(i + 1, i) for i in range(size - 1)])
-            halos[0] = lax.ppermute(got[2], "rng", [(i, i + 1) for i in range(size - 1)])
+            halos[3] = near_by(lax.ppermute(got[1], "rng", [(i + 1, i) for i in range(size - 1)]))
+            halos[0] = near_by(lax.ppermute(got[2], "rng", [(i, i + 1) for i in range(size - 1)]))
         mine = lax.all_to_all(got[0], "x", split_axis=0, concat_axis=0, tiled=True)
-        below = lax.ppermute(mine[3], "z", up)
-        above = lax.ppermute(mine[0], "z", down)
+        below = near_by(lax.ppermute(mine[3], "z", up))
+        above = near_by(lax.ppermute(mine[0], "z", down))
         units.append((below, mine, above))
     first = lax.axis_index("z").astype(jnp.int32) * 32 - 8
     tab = table(first.reshape(1), pairs_t)
@@ -467,7 +472,7 @@
         last = n == len(CHUNKS) - 1
         ins = coherence(True, tiles, tab, units[n][1:2], ins, (), last)
         outs = coherence(False, tiles, tab, units[n], outs, ins if last else (), last)
-    got = lax.all_to_all(outs, "z", split_axis=0, concat_axis=0, tiled=True)
+    got = near_by(lax.all_to_all(outs, "z", split_axis=0, concat_axis=0, tiled=True))
     series = solve(inv, got)
     return jnp.transpose(series.reshape(2, 2, 32, DATES), (0, 3, 1, 2))
 

time: 129 us -> 122 us (0.946)
  local copies, waits for them, and re-layouts: 6.29 us -> 2.41 us
  Pallas kernels: 58.9 us -> 55.3 us
    pallas_call x4, Pallas kernels: 29 us -> 25.1 us  [coherence(): pl.pallas_call(functools.partial(inner_kernel if inner else outer_kernel,...]
    unnamed x20 -> x6, local copies, waits for them, and re-layouts: 3.87 us -> 0.01 us
  transfers between devices with their start and end apart: 9 -> 9, of which waited for: 5 -> 5; matrix products, arithmetic and copies ran while one was open for 2% -> 2% of each run, Pallas kernels for 32% -> 31%
where the time goes in v1:
time: 122 us
  Pallas kernels  55.3 us (45%)
  waiting for transfers between devices  32.9 us (27%)
  starting transfers between devices  30.8 us (25%)
  local copies, waits for them, and re-layouts  2.41 us (2%)
    all_to_all x2, waiting for transfers between devices, per_device(): mine = lax.all_to_all(got[0], 'x', split_axis=0, concat_axis=0, tiled=True)  29 us
    pallas_call x4, Pallas kernels, coherence(): pl.pallas_call(functools.partial(inner_kernel if inner else outer_kernel,...  25.1 us
    pallas_call x2, Pallas kernels, resample(): pl.pallas_call(functools.partial(resample_kernel, tiles, needed, halo_in,...  18 us
    ppermute x2, starting transfers between devices, per_device(): above = near_by(lax.ppermute(mine[0], 'z', down))  11.8 us
    all_to_all x2, starting transfers between devices, per_device(): mine = lax.all_to_all(got[0], 'x', split_axis=0, concat_axis=0, tiled=True)  8.87 us
    pallas_call x1, Pallas kernels, inverse(): pl.pallas_call(inverse_kernel, out_shape=jax.ShapeDtypeStruct((DATES, DAT...  8.38 us
    all_to_all x1, starting transfers between devices, per_device(): lax.all_to_all(outs, 'z', split_axis=0, concat_axis=0, tiled=True)  4.64 us
    ppermute x1, starting transfers between devices, per_device(): lax.ppermute(got[1], 'rng', [(i + 1, i) for i in range(size - 1)])  3.64 us
  transfers between devices with their start and end apart: 9, of which 5 were waited for; matrix products, arithmetic and copies ran while one was open for 2% of the time, Pallas kernels for 31%

profile of v1, /device:TPU:16, one launch (start us, length us, event | category | flops | bytes accessed | tf_op | source)
XLA Modules:
  0.0 121.6 jit_solution(7724024842429187884)
XLA Ops:
  0.0 9.2 %shard_map.64 = (bf16[4,2,8,2,64,128]{5,4,3,2,1,0:T(8,128)(2,1)}, bf16[2,256,128]{2,1,0:T(8,128)(2,1)}, bf16[2,256,128]{2,1,0:T(8,128)(2,1)}) custom-call(s32[4,2,8]{2,1,0:T(2,128)} %bitcast.16, f32[8,8]{1,0:T(8,128)} %taps_ref.3, bf16[8,2,256,512]{3,2,1,0:T(8,128)(2,1)} %refs_3_.3, bf16[8,2,256,512]{3,2,1,0:T(8,128)(2,1)} %refs_3_.3, ...), custom_call_target="tpu_custom_call" | custom-call | tf_op jit(solution)/shard_map/pallas_call | solution.py:136
  9.2 0.0 copy-start.1
  9.2 4.4 %all-to-all-start.1 = ((bf16[4,2,8,2,64,128]{5,4,3,2,1,0:T(8,128)(2,1)}), bf16[4,2,8,2,64,128]{5,4,3,2,1,0:T(8,128)(2,1)S(1)}, u32[]{:S(2)}, u32[]{:S(2)}) async-start(bf16[4,2,8,2,64,128]{5,4,3,2,1,0:T(8,128)(2,1)} %get-tuple-element.16), calls=%async_computation.1 | async-start | bytes 4194304 | tf_op jit(solution)/shard_map/all_to_all | solution.py:463
  13.7 1.9 %collective-permute-start = (bf16[2,256,128]{2,1,0:T(8,128)(2,1)S(1)}, bf16[2,256,128]{2,1,0:T(8,128)(2,1)S(1)}, u32[]{:S(2)}, u32[]{:S(2)}) collective-permute-start(bf16[2,256,128]{2,1,0:T(8,128)(2,1)S(1)} %copy-done.2), channel_id=1, source_target_pairs={{0,1},{1,2},{2,3},{3,4},{4,5},{5,6},{6,7},{8,9},{9,10},{10,11},{11... | collective-permute-start | bytes 393224 | tf_op jit(solution)/shard_map/ppermute | solution.py:462
  15.6 3.6 %collective-permute-start.1 = (bf16[2,256,128]{2,1,0:T(8,128)(2,1)S(1)}, bf16[2,256,128]{2,1,0:T(8,128)(2,1)S(1)}, u32[]{:S(2)}, u32[]{:S(2)}) collective-permute-start(bf16[2,256,128]{2,1,0:T(8,128)(2,1)S(1)} %copy-done.1), channel_id=1, source_target_pairs={{1,0},{2,1},{3,2},{4,3},{5,4},{6,5},{7,6},{9,8},{10,9},{11,10},{12... | collective-permute-start | bytes 393224 | tf_op jit(solution)/shard_map/ppermute | solution.py:461
  19.2 0.7 collective-permute-done.refs_4_
  19.9 1.8 %collective-permute-done.1.refs_5_ = bf16[2,256,128]{2,1,0:T(8,128)(2,1)S(1)} collective-permute-done((bf16[2,256,128]{2,1,0:T(8,128)(2,1)S(1)}, bf16[2,256,128]{2,1,0:T(8,128)(2,1)S(1)}, u32[]{:S(2)}, u32[]{:S(2)}) %collective-permute-start.1) | collective-permute-done | bytes 131104 | tf_op jit(solution)/shard_map/ppermute | solution.py:461
  21.7 8.8 %shard_map.65 = bf16[4,2,8,2,64,128]{5,4,3,2,1,0:T(8,128)(2,1)} custom-call(s32[4,2,8]{2,1,0:T(2,128)} %bitcast.17, f32[8,8]{1,0:T(8,128)} %taps_ref.3, bf16[8,2,256,512]{3,2,1,0:T(8,128)(2,1)} %refs_3_.3, bf16[8,2,256,512]{3,2,1,0:T(8,128)(2,1)} %refs_3_.3, bf16[8,2,256,512]{3,2,1,0:T(8,128)(2,1)} %refs_3_.3, bf16[8,2,256,512]{3,2,1,0:T(8,128)(2,1)} %refs_3_.3, ...), custom_call_target="tpu_custom_call" | custom-call | tf_op jit(solution)/shard_map/pallas_call | solution.py:136
  30.5 9.5 %all-to-all-done.1.mine = bf16[4,2,8,2,64,128]{5,4,3,2,1,0:T(8,128)(2,1)S(1)} async-done(((bf16[4,2,8,2,64,128]{5,4,3,2,1,0:T(8,128)(2,1)}), bf16[4,2,8,2,64,128]{5,4,3,2,1,0:T(8,128)(2,1)S(1)}, u32[]{:S(2)}, u32[]{:S(2)}) %all-to-all-start.1) | async-done | bytes 2097184 | tf_op jit(solution)/shard_map/all_to_all | solution.py:463
  40.0 4.4 %all-to-all-start = ((bf16[4,2,8,2,64,128]{5,4,3,2,1,0:T(8,128)(2,1)}), bf16[4,2,8,2,64,128]{5,4,3,2,1,0:T(8,128)(2,1)}, u32[]{:S(2)}, u32[]{:S(2)}) async-start(bf16[4,2,8,2,64,128]{5,4,3,2,1,0:T(8,128)(2,1)} %shard_map.65), calls=%async_computation | async-start | bytes 4194304 | tf_op jit(solution)/shard_map/all_to_all | solution.py:463
  44.5 0.1 slice_bitcast_fusion
  44.6 5.9 %collective-permute-start.5 = (bf16[2,8,2,64,128]{4,3,2,1,0:T(8,128)(2,1)S(1)}, bf16[2,8,2,64,128]{4,3,2,1,0:T(8,128)(2,1)S(1)}, u32[]{:S(2)}, u32[]{:S(2)}) collective-permute-start(bf16[2,8,2,64,128]{4,3,2,1,0:T(8,128)(2,1)S(1)} %get-tuple-element.23), channel_id=1, source_target_pairs={{32,0},{64,32},{96,64},{128,96},{160,128},{192,160},{224,192},{0,2... | collective-permute-start | bytes 1572872 | tf_op jit(solution)/shard_map/ppermute | solution.py:465
  50.5 19.5 %all-to-all-done.mine = bf16[4,2,8,2,64,128]{5,4,3,2,1,0:T(8,128)(2,1)} async-done(((bf16[4,2,8,2,64,128]{5,4,3,2,1,0:T(8,128)(2,1)}), bf16[4,2,8,2,64,128]{5,4,3,2,1,0:T(8,128)(2,1)}, u32[]{:S(2)}, u32[]{:S(2)}) %all-to-all-start) | async-done | bytes 2097184 | tf_op jit(solution)/shard_map/all_to_all | solution.py:463
  70.0 2.3 %slice_bitcast_fusion.2 = (bf16[2,8,2,64,128]{4,3,2,1,0:T(8,128)(2,1)}, bf16[2,8,2,64,128]{4,3,2,1,0:T(8,128)(2,1)}) fusion(bf16[4,2,8,2,64,128]{5,4,3,2,1,0:T(8,128)(2,1)} %all-to-all-done.mine), kind=kLoop, calls=%fused_computation.2 | loop fusion | bytes 2097152 | tf_op jit(solution)/shard_map/squeeze | solution.py:465
  72.3 5.8 %collective-permute-start.3 = (bf16[2,8,2,64,128]{4,3,2,1,0:T(8,128)(2,1)}, bf16[2,8,2,64,128]{4,3,2,1,0:T(8,128)(2,1)S(1)}, u32[]{:S(2)}, u32[]{:S(2)}) collective-permute-start(bf16[2,8,2,64,128]{4,3,2,1,0:T(8,128)(2,1)} %get-tuple-element.25), channel_id=1, source_target_pairs={{32,0},{64,32},{96,64},{128,96},{160,128},{192,160},{224,192},{0,2... | collective-permute-start | bytes 1572872 | tf_op jit(solution)/shard_map/ppermute | solution.py:465
  78.1 2.0 %table.1.tab_ref = s32[32,128]{1,0:T(8,128)} custom-call(s32[1]{0:T(128)} %bitcast.1.first_ref, s32[2,1024]{1,0:T(2,128)} %bitcast.14), custom_call_target="tpu_custom_call" | custom-call | tf_op jit(solution)/shard_map/table/pallas_call | solution.py:164
  80.1 6.2 %shard_map.67 = (f32[512,128]{1,0:T(8,128)}, f32[256,128]{1,0:T(8,128)}) custom-call(s32[32,128]{1,0:T(8,128)} %table.1.tab_ref, bf16[4,2,8,2,64,128]{5,4,3,2,1,0:T(8,128)(2,1)} %copy-done), custom_call_target="tpu_custom_call" | custom-call | tf_op jit(solution)/shard_map/pallas_call | solution.py:408
  86.3 6.6 %shard_map.68 = (f32[384,128]{1,0:T(8,128)}, f32[256,128]{1,0:T(8,128)}) custom-call(s32[32,128]{1,0:T(8,128)} %table.1.tab_ref, bf16[4,2,8,2,64,128]{5,4,3,2,1,0:T(8,128)(2,1)} %all-to-all-done.mine, f32[512,128]{1,0:T(8,128)} %get-tuple-element.19.refs_0_, f32[256,128]{1,0:T(8,128)} %get-tuple-element.20.refs_1_), custom_call_target="tpu_custom_call" | custom-call | tf_op jit(solution)/shard_map/pallas_call | solution.py:408
  92.9 5.8 %shard_map.66 = (f32[512,128]{1,0:T(8,128)}, f32[128,128]{1,0:T(8,128)}) custom-call(s32[32,128]{1,0:T(8,128)} %table.1.tab_ref, bf16[2,8,2,64,128]{4,3,2,1,0:T(8,128)(2,1)S(1)} %collective-permute-done.4.below, bf16[4,2,8,2,64,128]{5,4,3,2,1,0:T(8,128)(2,1)} %copy-done, bf16[2,8,2,64,128]{4,3,2,1,0:T(8,128)(2,1)S(1)} %collective-permute-done.5.above), custom_call_target="tpu_custom_call" | custom-call | tf_op jit(solution)/shard_map/pallas_call | solution.py:408
  98.8 6.5 %shard_map.69 = f32[8,48,128]{2,1,0:T(8,128)} custom-call(s32[32,128]{1,0:T(8,128)} %table.1.tab_ref, bf16[2,8,2,64,128]{4,3,2,1,0:T(8,128)(2,1)S(1)} %collective-permute-done.2.below, bf16[4,2,8,2,64,128]{5,4,3,2,1,0:T(8,128)(2,1)} %all-to-all-done.mine, bf16[2,8,2,64,128]{4,3,2,1,0:T(8,128)(2,1)S(1)} %collective-permute-done.3.above, ...), custom_call_target="tpu_custom_call" | custom-call | tf_op jit(solution)/shard_map/pallas_call | solution.py:408
  105.2 4.6 %all-to-all-start.2 = ((f32[8,48,128]{2,1,0:T(8,128)}), f32[8,48,128]{2,1,0:T(8,128)S(1)}, u32[]{:S(2)}, u32[]{:S(2)}) async-start(f32[8,48,128]{2,1,0:T(8,128)} %shard_map.69), calls=%async_computation.2 | async-start | bytes 393216 | tf_op jit(solution)/shard_map/all_to_all | solution.py:475
  109.9 8.4 %inverse.1.inv_ref = f32[256,256]{1,0:T(8,128)} custom-call(s32[2,1024]{1,0:T(2,128)} %bitcast.15), custom_call_target="tpu_custom_call" | custom-call | tf_op jit(solution)/shard_map/inverse/pallas_call | solution.py:209
  118.3 1.4 %all-to-all-done.2.got_ref = f32[8,48,128]{2,1,0:T(8,128)S(1)} async-done(((f32[8,48,128]{2,1,0:T(8,128)}), f32[8,48,128]{2,1,0:T(8,128)S(1)}, u32[]{:S(2)}, u32[]{:S(2)}) %all-to-all-start.2) | async-done | bytes 196640 | tf_op jit(solution)/shard_map/all_to_all | solution.py:475
  119.7 1.9 %solve.1 = f32[128,256]{1,0:T(8,128)} custom-call(f32[256,256]{1,0:T(8,128)} %inverse.1.inv_ref, f32[8,48,128]{2,1,0:T(8,128)S(1)} %all-to-all-done.2.got_ref), custom_call_target="tpu_custom_call" | custom-call | tf_op jit(solution)/shard_map/solve/pallas_call | solution.py:436
  (11 shorter events, 0.0 us)
Async XLA Ops:
  9.2 4.5 %copy-start.2 = (bf16[2,256,128]{2,1,0:T(8,128)(2,1)S(1)}, bf16[2,256,128]{2,1,0:T(8,128)(2,1)}, u32[]{:S(2)}) copy-start(bf16[2,256,128]{2,1,0:T(8,128)(2,1)} %get-tuple-element.14) | copy-start | bytes 393220
  9.2 6.4 %copy-start.1 = (bf16[2,256,128]{2,1,0:T(8,128)(2,1)S(1)}, bf16[2,256,128]{2,1,0:T(8,128)(2,1)}, u32[]{:S(2)}) copy-start(bf16[2,256,128]{2,1,0:T(8,128)(2,1)} %get-tuple-element.15) | copy-start | bytes 393220
  9.2 30.8 %all-to-all-start.1 = ((bf16[4,2,8,2,64,128]{5,4,3,2,1,0:T(8,128)(2,1)}), bf16[4,2,8,2,64,128]{5,4,3,2,1,0:T(8,128)(2,1)S(1)}, u32[]{:S(2)}, u32[]{:S(2)}) async-start(bf16[4,2,8,2,64,128]{5,4,3,2,1,0:T(8,128)(2,1)} %get-tuple-element.16), calls=%async_computation.1 | async-start | bytes 4194304 | tf_op jit(solution)/shard_map/all_to_all | solution.py:463
  13.7 6.3 %collective-permute-start = (bf16[2,256,128]{2,1,0:T(8,128)(2,1)S(1)}, bf16[2,256,128]{2,1,0:T(8,128)(2,1)S(1)}, u32[]{:S(2)}, u32[]{:S(2)}) collective-permute-start(bf16[2,256,128]{2,1,0:T(8,128)(2,1)S(1)} %copy-done.2), channel_id=1, source_target_pairs={{0,1},{1,2},{2,3},{3,4},{4,5},{5,6},{6,7},{8,9},{9,10},{10,11},{11... | collective-permute-start | bytes 393224 | tf_op jit(solution)/shard_map/ppermute | solution.py:462
  15.6 6.1 %collective-permute-start.1 = (bf16[2,256,128]{2,1,0:T(8,128)(2,1)S(1)}, bf16[2,256,128]{2,1,0:T(8,128)(2,1)S(1)}, u32[]{:S(2)}, u32[]{:S(2)}) collective-permute-start(bf16[2,256,128]{2,1,0:T(8,128)(2,1)S(1)} %copy-done.1), channel_id=1, source_target_pairs={{1,0},{2,1},{3,2},{4,3},{5,4},{6,5},{7,6},{9,8},{10,9},{11,10},{12... | collective-permute-start | bytes 393224 | tf_op jit(solution)/shard_map/ppermute | solution.py:461
  40.0 4.5 %copy-start = (bf16[4,2,8,2,64,128]{5,4,3,2,1,0:T(8,128)(2,1)}, bf16[4,2,8,2,64,128]{5,4,3,2,1,0:T(8,128)(2,1)S(1)}, u32[]{:S(2)}) copy-start(bf16[4,2,8,2,64,128]{5,4,3,2,1,0:T(8,128)(2,1)S(1)} %all-to-all-done.1.mine) | copy-start | bytes 6291460
  40.0 30.0 %all-to-all-start = ((bf16[4,2,8,2,64,128]{5,4,3,2,1,0:T(8,128)(2,1)}), bf16[4,2,8,2,64,128]{5,4,3,2,1,0:T(8,128)(2,1)}, u32[]{:S(2)}, u32[]{:S(2)}) async-start(bf16[4,2,8,2,64,128]{5,4,3,2,1,0:T(8,128)(2,1)} %shard_map.65), calls=%async_computation | async-start | bytes 4194304 | tf_op jit(solution)/shard_map/all_to_all | solution.py:463
  44.6 48.3 %collective-permute-start.5 = (bf16[2,8,2,64,128]{4,3,2,1,0:T(8,128)(2,1)S(1)}, bf16[2,8,2,64,128]{4,3,2,1,0:T(8,128)(2,1)S(1)}, u32[]{:S(2)}, u32[]{:S(2)}) collective-permute-start(bf16[2,8,2,64,128]{4,3,2,1,0:T(8,128)(2,1)S(1)} %get-tuple-element.23), channel_id=1, source_target_pairs={{32,0},{64,32},{96,64},{128,96},{160,128},{192,160},{224,192},{0,2... | collective-permute-start | bytes 1572872 | tf_op jit(solution)/shard_map/ppermute | solution.py:465
  50.5 42.4 %collective-permute-start.4 = (bf16[2,8,2,64,128]{4,3,2,1,0:T(8,128)(2,1)S(1)}, bf16[2,8,2,64,128]{4,3,2,1,0:T(8,128)(2,1)S(1)}, u32[]{:S(2)}, u32[]{:S(2)}) collective-permute-start(bf16[2,8,2,64,128]{4,3,2,1,0:T(8,128)(2,1)S(1)} %get-tuple-element.24), channel_id=1, source_target_pairs={{0,32},{32,64},{64,96},{96,128},{128,160},{160,192},{192,224},{224... | collective-permute-start | bytes 1572872 | tf_op jit(solution)/shard_map/ppermute | solution.py:464
  72.3 26.5 %collective-permute-start.3 = (bf16[2,8,2,64,128]{4,3,2,1,0:T(8,128)(2,1)}, bf16[2,8,2,64,128]{4,3,2,1,0:T(8,128)(2,1)S(1)}, u32[]{:S(2)}, u32[]{:S(2)}) collective-permute-start(bf16[2,8,2,64,128]{4,3,2,1,0:T(8,128)(2,1)} %get-tuple-element.25), channel_id=1, source_target_pairs={{32,0},{64,32},{96,64},{128,96},{160,128},{192,160},{224,192},{0,2... | collective-permute-start | bytes 1572872 | tf_op jit(solution)/shard_map/ppermute | solution.py:465
  78.1 20.6 %collective-permute-start.2 = (bf16[2,8,2,64,128]{4,3,2,1,0:T(8,128)(2,1)}, bf16[2,8,2,64,128]{4,3,2,1,0:T(8,128)(2,1)S(1)}, u32[]{:S(2)}, u32[]{:S(2)}) collective-permute-start(bf16[2,8,2,64,128]{4,3,2,1,0:T(8,128)(2,1)} %get-tuple-element.26), channel_id=1, source_target_pairs={{0,32},{32,64},{64,96},{96,128},{128,160},{160,192},{192,224},{224... | collective-permute-start | bytes 1572872 | tf_op jit(solution)/shard_map/ppermute | solution.py:464
  105.2 14.4 %all-to-all-start.2 = ((f32[8,48,128]{2,1,0:T(8,128)}), f32[8,48,128]{2,1,0:T(8,128)S(1)}, u32[]{:S(2)}, u32[]{:S(2)}) async-start(f32[8,48,128]{2,1,0:T(8,128)} %shard_map.69), calls=%async_computation.2 | async-start | bytes 393216 | tf_op jit(solution)/shard_map/all_to_all | solution.py:475

commit v2 on v1

--- a/solution.py
+++ b/solution.py
@@ -49,12 +49,12 @@
     return (row - shift == np.arange(256)).astype(np.float32)
 
 
-def resample_kernel(tiles, needed, halo_in, pack, off_ref, taps_ref, *refs):
+def resample_kernel(tiles, needed, halo_in, pack, off_ref, taps_ref, x_ref, *refs):
     refs = list(refs)
     data = {t: refs.pop(0) for t in needed}
     halo = {t: refs.pop(0) for t in halo_in}
     perm = refs.pop(0)
-    out = refs.pop(0)
+    outs = [refs.pop(0) for _ in range(4)]
     packs = [refs.pop(0) for _ in range(2)] if pack else None
     i = pl.program_id(0)
     if pack:
@@ -111,13 +111,17 @@
                 wide = dot(lhs, weights)
                 parts.append((wide[:, :128] + wide[:, 128:]).astype(BF16))
             both = jnp.concatenate(parts, axis=1)
-            moved = dot(perm[row_shift + 2], both).astype(BF16)
+            order = [
+                perm[row_shift + 2, pl.ds(pl.multiple_of(64 * ((x_ref[0] + g) & 3), 64), 64), :]
+                for g in range(4)
+            ]
+            moved = dot(jnp.concatenate(order, axis=0), both).astype(BF16)
             for g in range(4):
                 for c in range(2):
-                    out[g, n, e, c] = moved[64 * g : 64 * g + 64, 128 * c : 128 * c + 128]
-
-
-def resample(tiles, slc, halos, offs, taps, pack):
+                    outs[g][n, e, c] = moved[64 * g : 64 * g + 64, 128 * c : 128 * c + 128]
+
+
+def resample(tiles, slc, halos, offs, taps, x, pack):
     needed = {s for t in tiles for s in (t - 1, t, t + 1) if 0 <= s < 4}
     needed = sorted(needed | {0, 3} if pack else needed)
     halo_in = [t for t in tiles if t in (0, 3)]
@@ -128,8 +132,8 @@
         for t in needed
     ] + [pl.BlockSpec(memory_space=pltpu.VMEM)] * len(halo_in)
     in_specs.append(pl.BlockSpec((5, 256, 256), lambda d, *_: (0, 0, 0)))
-    out_specs = [pl.BlockSpec((4, count, STEP, 2, 64, 128), lambda d, *_: (0, 0, d, 0, 0, 0))]
-    out_shape = [jax.ShapeDtypeStruct((4, count, UNIT, 2, 64, 128), BF16)]
+    out_specs = [pl.BlockSpec((count, STEP, 2, 64, 128), lambda d, *_: (0, d, 0, 0, 0))] * 4
+    out_shape = [jax.ShapeDtypeStruct((count, UNIT, 2, 64, 128), BF16)] * 4
     if pack:
         out_specs += [whole] * 2
         out_shape += [jax.ShapeDtypeStruct((2, 256, 128), BF16)] * 2
@@ -137,12 +141,12 @@
         functools.partial(resample_kernel, tiles, needed, halo_in, pack),
         out_shape=out_shape,
         grid_spec=pltpu.PrefetchScalarGridSpec(
-            num_scalar_prefetch=2,
+            num_scalar_prefetch=3,
             grid=(UNIT // STEP,),
             in_specs=in_specs,
             out_specs=out_specs,
         ),
-    )(offs, taps, *([slc] * len(needed)), *[halos[t] for t in halo_in], jnp.asarray(row_moves(), BF16))
+    )(offs, taps, x, *([slc] * len(needed)), *[halos[t] for t in halo_in], jnp.asarray(row_moves(), BF16))
 
 
 def table_kernel(first_ref, pairs_ref, out_ref):
@@ -281,11 +285,12 @@
                 at = pl.ds(pl.multiple_of(i * 32 + 16 * half, 16), 16)
                 for g in range(4):
                     v = jnp.concatenate([got[0][g], got[1][g]], axis=0)
-                    sums[at, 128 * g : 128 * g + 128] = v.astype(BF16)
+                    for m, part in enumerate(split(v)):
+                        sums[m, at, 128 * g : 128 * g + 128] = part
             return 0
 
         lax.fori_loop(0, HALF, pair_step, 0, unroll=UNROLL)
-        looks = dot(sums[...], sel)
+        looks = dot(sums[0], sel) + dot(sums[1], sel)
         if n > 0:
             looks = looks + raw[...]
         elif before:
@@ -322,14 +327,15 @@
     rhs[SLOTS] = (rhs[0] + rhs[1]) + (rhs[2] + rhs[3]) + rhs[SLOTS]
 
 
-def inner_kernel(tiles, first, last, tab_ref, mine, *refs):
+def inner_kernel(tiles, first, last, tab_ref, *refs):
     refs = list(refs)
+    mine = [refs.pop(0) for _ in range(4)]
     before = () if first else (refs.pop(0), refs.pop(0))
     if last:
         rhs_out, power, win, sums, squares, sem, raw, whole, rhs = refs
     else:
         raw, power, win, sums, squares, sem = refs
-    copies = copies_of([(u + 1, mine.at[u]) for u in range(4)], win, sem, len(tiles))
+    copies = copies_of([(u + 1, mine[u]) for u in range(4)], win, sem, len(tiles))
 
     def place(i):
         return i + INNER[0]
@@ -344,16 +350,16 @@
         rhs_out[...] = rhs[SLOTS]
 
 
-def outer_kernel(tiles, first, last, tab_ref, below, mine, above, *refs):
+def outer_kernel(tiles, first, last, tab_ref, *refs):
     refs = list(refs)
+    units = [refs.pop(0) for _ in range(6)]
     before = () if first else (refs.pop(0), refs.pop(0))
     if last:
         inner_rhs, inner_power = refs.pop(0), refs.pop(0)
         out_ref, win, sums, squares, sem, raw, power, whole, rhs = refs
     else:
         raw, power, win, sums, squares, sem = refs
-    sources = [(u + 1, mine.at[u]) for u in range(4)] + [(0, below), (5, above)]
-    copies = copies_of(sources, win, sem, len(tiles))
+    copies = copies_of(list(enumerate(units)), win, sem, len(tiles))
 
     def place(i):
         return jnp.where(i < INNER[0], i, i + INNER[1] - INNER[0])
@@ -389,7 +395,7 @@
     power = jax.ShapeDtypeStruct((rows, 128), F32)
     scratch = [
         pltpu.VMEM((count, WINDOW, 2, 64, 128), BF16),
-        pltpu.VMEM((RAW, 512), BF16),
+        pltpu.VMEM((2, RAW, 512), BF16),
         pltpu.VMEM((2, rows, 256), BF16),
         pltpu.SemaphoreType.DMA((count, 6)),
     ]
@@ -409,7 +415,7 @@
         functools.partial(inner_kernel if inner else outer_kernel, tiles, not before, last),
         out_shape=outs,
         in_specs=[pl.BlockSpec(memory_space=pltpu.SMEM)]
-        + [vmem if len(units) == 3 and u != 1 else pl.BlockSpec(memory_space=pl.ANY) for u in range(len(units))]
+        + [vmem if not inner and u in (0, 5) else pl.BlockSpec(memory_space=pl.ANY) for u in range(len(units))]
         + [vmem] * len((*before, *extra)),
         out_specs=[vmem] * 2 if isinstance(outs, list) else vmem,
         scratch_shapes=scratch,
@@ -443,34 +449,63 @@
     )(inv, got)
 
 
+def arrange_kernel(x_ref, *refs):
+    sources, outs = refs[:4], refs[4:]
+    for u in range(4):
+        for away in range(4):
+
+            @pl.when(((u - x_ref[0]) & 3) == away)
+            def _():
+                outs[u][...] = sources[away][...]
+
+
+def arrange(x, pieces):
+    vmem = pl.BlockSpec(memory_space=pltpu.VMEM)
+    return pl.pallas_call(
+        arrange_kernel,
+        out_shape=[jax.ShapeDtypeStruct(p.shape, p.dtype) for p in pieces],
+        in_specs=[pl.BlockSpec(memory_space=pltpu.SMEM)] + [vmem] * 4,
+        out_specs=[vmem] * 4,
+    )(x, *pieces)
+
+
 def near_by(v):
     return pltpu.with_memory_space_constraint(v, pltpu.VMEM)
 
 
+def shift(v, axis, step):
+    size = lax.axis_size(axis)
+    return lax.ppermute(v, axis, [(i, (i + step) % size) for i in range(size)])
+
+
 def per_device(slc, offsets, taps, pairs):
+    x = lax.axis_index("x").astype(jnp.int32)
+    first = lax.axis_index("z").astype(jnp.int32) * 32 - 8
+    xs = x.reshape(1)
     pairs_t = pairs.T
     offs = jnp.transpose(offsets, (1, 2, 0))
     halos = {}
     units = []
-    up = [(z, (z + 1) % 8) for z in range(8)]
-    down = [(j, i) for i, j in up]
     for n, tiles in enumerate(CHUNKS):
-        got = resample(tiles, slc, halos, offs, taps, n == 0)
+        got = resample(tiles, slc, halos, offs, taps, xs, n == 0)
         if n == 0:
             size = lax.axis_size("rng")
-            halos[3] = near_by(lax.ppermute(got[1], "rng", [(i + 1, i) for i in range(size - 1)]))
-            halos[0] = near_by(lax.ppermute(got[2], "rng", [(i, i + 1) for i in range(size - 1)]))
-        mine = lax.all_to_all(got[0], "x", split_axis=0, concat_axis=0, tiled=True)
-        below = near_by(lax.ppermute(mine[3], "z", up))
-        above = near_by(lax.ppermute(mine[0], "z", down))
-        units.append((below, mine, above))
-    first = lax.axis_index("z").astype(jnp.int32) * 32 - 8
+            halos[3] = near_by(lax.ppermute(got[4], "rng", [(i + 1, i) for i in range(size - 1)]))
+            halos[0] = near_by(lax.ppermute(got[5], "rng", [(i, i + 1) for i in range(size - 1)]))
+        own, ahead, across, behind = got[:4]
+        plus2 = near_by(shift(across, "x", 2))
+        minus1 = near_by(shift(ahead, "x", 1))
+        plus1 = near_by(shift(behind, "x", -1))
+        mine = arrange(xs, (own, plus1, plus2, minus1))
+        below = near_by(shift(mine[3], "z", 1))
+        above = near_by(shift(mine[0], "z", -1))
+        units.append((below, *mine, above))
     tab = table(first.reshape(1), pairs_t)
     inv = inverse(pairs_t)
     ins, outs = (), ()
     for n, tiles in enumerate(CHUNKS):
         last = n == len(CHUNKS) - 1
-        ins = coherence(True, tiles, tab, units[n][1:2], ins, (), last)
+        ins = coherence(True, tiles, tab, units[n][1:5], ins, (), last)
         outs = coherence(False, tiles, tab, units[n], outs, ins if last else (), last)
     got = near_by(lax.all_to_all(outs, "z", split_axis=0, concat_axis=0, tiled=True))
     series = solve(inv, got)

time: 122 us -> 125 us (1.025)
  Pallas kernels: 55.3 us -> 64.3 us
  waiting for transfers between devices: 32.9 us -> 28.8 us
  local copies, waits for them, and re-layouts: 2.41 us -> 0 us
    all_to_all x2 -> x0, waiting for transfers between devices: 29 us -> none  [per_device(): mine = lax.all_to_all(got[0], 'x', split_axis=0, concat_axis=0, tiled=True)]
    ppermute x6 -> x12, waiting for transfers between devices: 2.51 us -> 27.1 us  [the longest x10 26.1 us: shift(): return lax.ppermute(v, axis, [(i, (i + step) % size) for i in range(size)])]
    all_to_all x2 -> x0, starting transfers between devices: 8.87 us -> none  [per_device(): mine = lax.all_to_all(got[0], 'x', split_axis=0, concat_axis=0, tiled=True)]
    ppermute x6 -> x12, starting transfers between devices: 17.3 us -> 24.7 us  [the longest x10 19.2 us: shift(): return lax.ppermute(v, axis, [(i, (i + step) % size) for i in range(size)])]
    pallas_call x0 -> x2, Pallas kernels: none -> 5.25 us  [arrange(): pl.pallas_call(arrange_kernel, out_shape=[jax.ShapeDtypeStruct(p.shape, p...]
    pallas_call x4, Pallas kernels: 25.1 us -> 28.7 us  [coherence(): pl.pallas_call(functools.partial(inner_kernel if inner else outer_kernel,...]
    squeeze x2 -> x0, local copies, waits for them, and re-layouts: 2.39 us -> none  [per_device(): above = near_by(lax.ppermute(mine[0], 'z', down))]
  transfers between devices with their start and end apart: 9 -> 13, of which waited for: 5 -> 6; matrix products, arithmetic and copies ran while one was open for 2% -> 0% of each run, Pallas kernels for 31% -> 37%
where the time goes in v2:
time: 125 us; the launch traced here: 124 us
  Pallas kernels  64.3 us (51%)
  starting transfers between devices  30.6 us (24%)
  waiting for transfers between devices  28.8 us (23%)
    pallas_call x4, Pallas kernels, coherence(): pl.pallas_call(functools.partial(inner_kernel if inner else outer_kernel,...  28.7 us
    ppermute x10, waiting for transfers between devices, shift(): return lax.ppermute(v, axis, [(i, (i + step) % size) for i in range(size)])  26.1 us
    ppermute x10, starting transfers between devices, shift(): return lax.ppermute(v, axis, [(i, (i + step) % size) for i in range(size)])  19.2 us
    pallas_call x2, Pallas kernels, resample(): pl.pallas_call(functools.partial(resample_kernel, tiles, needed, halo_in,...  18.1 us
    pallas_call x1, Pallas kernels, inverse(): pl.pallas_call(inverse_kernel, out_shape=jax.ShapeDtypeStruct((DATES, DAT...  8.38 us
    all_to_all x1, starting transfers between devices, per_device(): lax.all_to_all(outs, 'z', split_axis=0, concat_axis=0, tiled=True)  5.86 us
    pallas_call x2, Pallas kernels, arrange(): pl.pallas_call(arrange_kernel, out_shape=[jax.ShapeDtypeStruct(p.shape, p...  5.25 us
    ppermute x1, starting transfers between devices, per_device(): lax.ppermute(got[4], 'rng', [(i + 1, i) for i in range(size - 1)])  3.64 us
  transfers between devices with their start and end apart: 13, of which 6 were waited for; matrix products, arithmetic and copies ran while one was open for 0% of the time, Pallas kernels for 37%

profile of v2, /device:TPU:16, one launch (start us, length us, event | category | flops | bytes accessed | tf_op | source)
XLA Modules:
  0.0 123.8 jit_solution(4019748952916408778)
XLA Ops:
  0.0 9.3 %shard_map.64 = (bf16[2,8,2,64,128]{4,3,2,1,0:T(8,128)(2,1)}, bf16[2,8,2,64,128]{4,3,2,1,0:T(8,128)(2,1)}, bf16[2,8,2,64,128]{4,3,2,1,0:T(8,128)(2,1)}, bf16[2,8...) custom-call(s32[4,2,8]{2,1,0:T(2,128)} %bitcast.9, f32[8,8]{1,0:T(8,128)} %taps_ref.3, ...), custom_call_target="tpu_custom_call" | custom-call | tf_op jit(solution)/shard_map/pallas_call | solution.py:140
  9.3 2.8 %collective-permute-start.7 = (bf16[2,8,2,64,128]{4,3,2,1,0:T(8,128)(2,1)}, bf16[2,8,2,64,128]{4,3,2,1,0:T(8,128)(2,1)S(1)}, u32[]{:S(2)}, u32[]{:S(2)}) collective-permute-start(bf16[2,8,2,64,128]{4,3,2,1,0:T(8,128)(2,1)} %get-tuple-element.40), channel_id=1, source_target_pairs={{0,24},{8,0},{16,8},{24,16},{1,25},{9,1},{17,9},{25,17},{2,26},{10... | collective-permute-start | bytes 1572872 | tf_op jit(solution)/shard_map/ppermute | solution.py:478
  12.1 1.9 %collective-permute-start = (bf16[2,256,128]{2,1,0:T(8,128)(2,1)}, bf16[2,256,128]{2,1,0:T(8,128)(2,1)S(1)}, u32[]{:S(2)}, u32[]{:S(2)}) collective-permute-start(bf16[2,256,128]{2,1,0:T(8,128)(2,1)} %get-tuple-element.29), channel_id=1, source_target_pairs={{0,1},{1,2},{2,3},{3,4},{4,5},{5,6},{6,7},{8,9},{9,10},{10,11},{11... | collective-permute-start | bytes 393224 | tf_op jit(solution)/shard_map/ppermute | solution.py:494
  14.0 3.6 %collective-permute-start.1 = (bf16[2,256,128]{2,1,0:T(8,128)(2,1)}, bf16[2,256,128]{2,1,0:T(8,128)(2,1)S(1)}, u32[]{:S(2)}, u32[]{:S(2)}) collective-permute-start(bf16[2,256,128]{2,1,0:T(8,128)(2,1)} %get-tuple-element.30), channel_id=1, source_target_pairs={{1,0},{2,1},{3,2},{4,3},{5,4},{6,5},{7,6},{9,8},{10,9},{11,10},{12... | collective-permute-start | bytes 393224 | tf_op jit(solution)/shard_map/ppermute | solution.py:493
  20.5 8.8 %shard_map.65 = (bf16[2,8,2,64,128]{4,3,2,1,0:T(8,128)(2,1)}, bf16[2,8,2,64,128]{4,3,2,1,0:T(8,128)(2,1)}, bf16[2,8,2,64,128]{4,3,2,1,0:T(8,128)(2,1)}, bf16[2,8,2,64,128]{4,3,2,1,0:T(8,128)(2,1)}) custom-call(s32[4,2,8]{2,1,0:T(2,128)} %bitcast.10, f32[8,8]{1,0:T(8,128)} %taps_ref.3, s32[1]{0:T(128)} %bitcast.2.x_ref, bf16[8,2,256,512]{3,2,1,0:T(8,128)(2,1)} %refs_3_.3, ...), custom_call_target="tpu_custom_call" | custom-call | tf_op jit(solution)/shard_map/pallas_call | solution.py:140
  32.1 3.8 %collective-permute-done.7.refs_1_ = bf16[2,8,2,64,128]{4,3,2,1,0:T(8,128)(2,1)S(1)} collective-permute-done((bf16[2,8,2,64,128]{4,3,2,1,0:T(8,128)(2,1)}, bf16[2,8,2,64,128]{4,3,2,1,0:T(8,128)(2,1)S(1)}, u32[]{:S(2)}, u32[]{:S(2)}) %collective-permute-start.7) | collective-permute-done | bytes 524320 | tf_op jit(solution)/shard_map/ppermute | solution.py:478
  36.0 9.6 %collective-permute-done.9.refs_3_ = bf16[2,8,2,64,128]{4,3,2,1,0:T(8,128)(2,1)S(1)} collective-permute-done((bf16[2,8,2,64,128]{4,3,2,1,0:T(8,128)(2,1)}, bf16[2,8,2,64,128]{4,3,2,1,0:T(8,128)(2,1)S(1)}, u32[]{:S(2)}, u32[]{:S(2)}) %collective-permute-start.9) | collective-permute-done | bytes 524320 | tf_op jit(solution)/shard_map/ppermute | solution.py:478
  45.6 2.6 %shard_map.67 = (bf16[2,8,2,64,128]{4,3,2,1,0:T(8,128)(2,1)}, bf16[2,8,2,64,128]{4,3,2,1,0:T(8,128)(2,1)}, bf16[2,8,2,64,128]{4,3,2,1,0:T(8,128)(2,1)}, bf16[2,8,2,64,128]{4,3,2,1,0:T(8,128)(2,1)}) custom-call(s32[1]{0:T(128)} %bitcast.2.x_ref, bf16[2,8,2,64,128]{4,3,2,1,0:T(8,128)(2,1)} %get-tuple-element.39.refs_0_, ...), custom_call_target="tpu_custom_call" | custom-call | tf_op jit(solution)/shard_map/pallas_call | solution.py:464
  48.2 1.9 %collective-permute-start.10 = (bf16[2,8,2,64,128]{4,3,2,1,0:T(8,128)(2,1)}, bf16[2,8,2,64,128]{4,3,2,1,0:T(8,128)(2,1)S(1)}, u32[]{:S(2)}, u32[]{:S(2)}) collective-permute-start(bf16[2,8,2,64,128]{4,3,2,1,0:T(8,128)(2,1)} %get-tuple-element.43.refs_4_.refs_3_), channel_id=1, source_target_pairs={{0,32},{32,64},{64,96},{96,128},{128,160},{160,192},{192,224},{224... | collective-permute-start | bytes 1572872 | tf_op jit(solution)/shard_map/ppermute | solution.py:478
  50.1 3.9 %collective-permute-start.11 = (bf16[2,8,2,64,128]{4,3,2,1,0:T(8,128)(2,1)}, bf16[2,8,2,64,128]{4,3,2,1,0:T(8,128)(2,1)S(1)}, u32[]{:S(2)}, u32[]{:S(2)}) collective-permute-start(bf16[2,8,2,64,128]{4,3,2,1,0:T(8,128)(2,1)} %get-tuple-element.44.refs_1_.refs_0_), channel_id=1, source_target_pairs={{0,224},{32,0},{64,32},{96,64},{128,96},{160,128},{192,160},{224,1... | collective-permute-start | bytes 1572872 | tf_op jit(solution)/shard_map/ppermute | solution.py:478
  54.1 3.2 %collective-permute-done.2.refs_1_ = bf16[2,8,2,64,128]{4,3,2,1,0:T(8,128)(2,1)S(1)} collective-permute-done((bf16[2,8,2,64,128]{4,3,2,1,0:T(8,128)(2,1)}, bf16[2,8,2,64,128]{4,3,2,1,0:T(8,128)(2,1)S(1)}, u32[]{:S(2)}, u32[]{:S(2)}) %collective-permute-start.2) | collective-permute-done | bytes 524320 | tf_op jit(solution)/shard_map/ppermute | solution.py:478
  57.3 9.3 %collective-permute-done.4.refs_3_ = bf16[2,8,2,64,128]{4,3,2,1,0:T(8,128)(2,1)S(1)} collective-permute-done((bf16[2,8,2,64,128]{4,3,2,1,0:T(8,128)(2,1)}, bf16[2,8,2,64,128]{4,3,2,1,0:T(8,128)(2,1)S(1)}, u32[]{:S(2)}, u32[]{:S(2)}) %collective-permute-start.4) | collective-permute-done | bytes 524320 | tf_op jit(solution)/shard_map/ppermute | solution.py:478
  66.7 2.6 %shard_map.66 = (bf16[2,8,2,64,128]{4,3,2,1,0:T(8,128)(2,1)}, bf16[2,8,2,64,128]{4,3,2,1,0:T(8,128)(2,1)}, bf16[2,8,2,64,128]{4,3,2,1,0:T(8,128)(2,1)}, bf16[2,8,2,64,128]{4,3,2,1,0:T(8,128)(2,1)}) custom-call(s32[1]{0:T(128)} %bitcast.2.x_ref, bf16[2,8,2,64,128]{4,3,2,1,0:T(8,128)(2,1)} %get-tuple-element.31.refs_0_, ...), custom_call_target="tpu_custom_call" | custom-call | tf_op jit(solution)/shard_map/pallas_call | solution.py:464
  69.3 1.9 %collective-permute-start.5 = (bf16[2,8,2,64,128]{4,3,2,1,0:T(8,128)(2,1)}, bf16[2,8,2,64,128]{4,3,2,1,0:T(8,128)(2,1)S(1)}, u32[]{:S(2)}, u32[]{:S(2)}) collective-permute-start(bf16[2,8,2,64,128]{4,3,2,1,0:T(8,128)(2,1)} %get-tuple-element.35.refs_3_.refs_4_), channel_id=1, source_target_pairs={{0,32},{32,64},{64,96},{96,128},{128,160},{160,192},{192,224},{224... | collective-permute-start | bytes 1572872 | tf_op jit(solution)/shard_map/ppermute | solution.py:478
  71.2 3.9 %collective-permute-start.6 = (bf16[2,8,2,64,128]{4,3,2,1,0:T(8,128)(2,1)}, bf16[2,8,2,64,128]{4,3,2,1,0:T(8,128)(2,1)S(1)}, u32[]{:S(2)}, u32[]{:S(2)}) collective-permute-start(bf16[2,8,2,64,128]{4,3,2,1,0:T(8,128)(2,1)} %get-tuple-element.36.refs_0_.refs_1_), channel_id=1, source_target_pairs={{0,224},{32,0},{64,32},{96,64},{128,96},{160,128},{192,160},{224,1... | collective-permute-start | bytes 1572872 | tf_op jit(solution)/shard_map/ppermute | solution.py:478
  75.2 2.0 %table.1.tab_ref = s32[32,128]{1,0:T(8,128)} custom-call(s32[1]{0:T(128)} %bitcast.1.first_ref, s32[2,1024]{1,0:T(2,128)} %bitcast.7), custom_call_target="tpu_custom_call" | custom-call | tf_op jit(solution)/shard_map/table/pallas_call | solution.py:168
  77.1 7.1 %shard_map.69 = (f32[512,128]{1,0:T(8,128)}, f32[256,128]{1,0:T(8,128)}) custom-call(s32[32,128]{1,0:T(8,128)} %table.1.tab_ref, bf16[2,8,2,64,128]{4,3,2,1,0:T(8,128)(2,1)} %get-tuple-element.44.refs_1_.refs_0_, bf16[2,8,2,64,128]{4,3,2,1,0:T(8,128)(2,1)} %get-tuple-element.45.refs_2_.refs_1_, ...), custom_call_target="tpu_custom_call" | custom-call | tf_op jit(solution)/shard_map/pallas_call | solution.py:414
  84.2 7.6 %shard_map.70 = (f32[384,128]{1,0:T(8,128)}, f32[256,128]{1,0:T(8,128)}) custom-call(s32[32,128]{1,0:T(8,128)} %table.1.tab_ref, bf16[2,8,2,64,128]{4,3,2,1,0:T(8,128)(2,1)} %get-tuple-element.36.refs_0_.refs_1_, bf16[2,8,2,64,128]{4,3,2,1,0:T(8,128)(2,1)} %get-tuple-element.37.refs_1_.refs_2_, ...), custom_call_target="tpu_custom_call" | custom-call | tf_op jit(solution)/shard_map/pallas_call | solution.py:414
  91.8 6.7 %shard_map.68 = (f32[512,128]{1,0:T(8,128)}, f32[128,128]{1,0:T(8,128)}) custom-call(s32[32,128]{1,0:T(8,128)} %table.1.tab_ref, bf16[2,8,2,64,128]{4,3,2,1,0:T(8,128)(2,1)S(1)} %collective-permute-done.10.refs_0_, bf16[2,8,2,64,128]{4,3,2,1,0:T(8,128)(2,1)} %get-tuple-element.44.refs_1_.refs_0_, ...), custom_call_target="tpu_custom_call" | custom-call | tf_op jit(solution)/shard_map/pallas_call | solution.py:414
  98.6 7.3 %shard_map.71 = f32[8,48,128]{2,1,0:T(8,128)} custom-call(s32[32,128]{1,0:T(8,128)} %table.1.tab_ref, bf16[2,8,2,64,128]{4,3,2,1,0:T(8,128)(2,1)S(1)} %collective-permute-done.5.refs_0_, bf16[2,8,2,64,128]{4,3,2,1,0:T(8,128)(2,1)} %get-tuple-element.36.refs_0_.refs_1_, bf16[2,8,2,64,128]{4,3,2,1,0:T(8,128)(2,1)} %get-tuple-element.37.refs_1_.refs_2_, ...), custom_call_target="tpu_custom_call" | custom-call | tf_op jit(solution)/shard_map/pallas_call | solution.py:414
  105.9 5.9 %all-to-all-start = ((f32[8,48,128]{2,1,0:T(8,128)}), f32[8,48,128]{2,1,0:T(8,128)S(1)}, u32[]{:S(2)}, u32[]{:S(2)}) async-start(f32[8,48,128]{2,1,0:T(8,128)} %shard_map.71), calls=%async_computation | async-start | bytes 393216 | tf_op jit(solution)/shard_map/all_to_all | solution.py:510
  111.8 8.4 %inverse.1.inv_ref = f32[256,256]{1,0:T(8,128)} custom-call(s32[2,1024]{1,0:T(2,128)} %bitcast.8), custom_call_target="tpu_custom_call" | custom-call | tf_op jit(solution)/shard_map/inverse/pallas_call | solution.py:213
  120.1 1.7 %all-to-all-done.got_ref = f32[8,48,128]{2,1,0:T(8,128)S(1)} async-done(((f32[8,48,128]{2,1,0:T(8,128)}), f32[8,48,128]{2,1,0:T(8,128)S(1)}, u32[]{:S(2)}, u32[]{:S(2)}) %all-to-all-start) | async-done | bytes 196640 | tf_op jit(solution)/shard_map/all_to_all | solution.py:510
  121.9 1.9 %solve.1 = f32[128,256]{1,0:T(8,128)} custom-call(f32[256,256]{1,0:T(8,128)} %inverse.1.inv_ref, f32[8,48,128]{2,1,0:T(8,128)S(1)} %all-to-all-done.got_ref), custom_call_target="tpu_custom_call" | custom-call | tf_op jit(solution)/shard_map/solve/pallas_call | solution.py:442
  (13 shorter events, 5.7 us)
Async XLA Ops:
  9.3 26.7 %collective-permute-start.7 = (bf16[2,8,2,64,128]{4,3,2,1,0:T(8,128)(2,1)}, bf16[2,8,2,64,128]{4,3,2,1,0:T(8,128)(2,1)S(1)}, u32[]{:S(2)}, u32[]{:S(2)}) collective-permute-start(bf16[2,8,2,64,128]{4,3,2,1,0:T(8,128)(2,1)} %get-tuple-element.40), channel_id=1, source_target_pairs={{0,24},{8,0},{16,8},{24,16},{1,25},{9,1},{17,9},{25,17},{2,26},{10... | collective-permute-start | bytes 1572872 | tf_op jit(solution)/shard_map/ppermute | solution.py:478
  12.1 7.4 %collective-permute-start = (bf16[2,256,128]{2,1,0:T(8,128)(2,1)}, bf16[2,256,128]{2,1,0:T(8,128)(2,1)S(1)}, u32[]{:S(2)}, u32[]{:S(2)}) collective-permute-start(bf16[2,256,128]{2,1,0:T(8,128)(2,1)} %get-tuple-element.29), channel_id=1, source_target_pairs={{0,1},{1,2},{2,3},{3,4},{4,5},{5,6},{6,7},{8,9},{9,10},{10,11},{11... | collective-permute-start | bytes 393224 | tf_op jit(solution)/shard_map/ppermute | solution.py:494
  14.0 6.5 %collective-permute-start.1 = (bf16[2,256,128]{2,1,0:T(8,128)(2,1)}, bf16[2,256,128]{2,1,0:T(8,128)(2,1)S(1)}, u32[]{:S(2)}, u32[]{:S(2)}) collective-permute-start(bf16[2,256,128]{2,1,0:T(8,128)(2,1)} %get-tuple-element.30), channel_id=1, source_target_pairs={{1,0},{2,1},{3,2},{4,3},{5,4},{6,5},{7,6},{9,8},{10,9},{11,10},{12... | collective-permute-start | bytes 393224 | tf_op jit(solution)/shard_map/ppermute | solution.py:493
  17.7 18.3 %collective-permute-start.8 = (bf16[2,8,2,64,128]{4,3,2,1,0:T(8,128)(2,1)}, bf16[2,8,2,64,128]{4,3,2,1,0:T(8,128)(2,1)S(1)}, u32[]{:S(2)}, u32[]{:S(2)}) collective-permute-start(bf16[2,8,2,64,128]{4,3,2,1,0:T(8,128)(2,1)} %get-tuple-element.41), channel_id=1, source_target_pairs={{0,16},{8,24},{16,0},{24,8},{1,17},{9,25},{17,1},{25,9},{2,18},{10... | collective-permute-start | bytes 1572872 | tf_op jit(solution)/shard_map/ppermute | solution.py:478
  18.6 27.0 %collective-permute-start.9 = (bf16[2,8,2,64,128]{4,3,2,1,0:T(8,128)(2,1)}, bf16[2,8,2,64,128]{4,3,2,1,0:T(8,128)(2,1)S(1)}, u32[]{:S(2)}, u32[]{:S(2)}) collective-permute-start(bf16[2,8,2,64,128]{4,3,2,1,0:T(8,128)(2,1)} %get-tuple-element.42), channel_id=1, source_target_pairs={{0,8},{8,16},{16,24},{24,0},{1,9},{9,17},{17,25},{25,1},{2,10},{10... | collective-permute-start | bytes 1572872 | tf_op jit(solution)/shard_map/ppermute | solution.py:478
  29.3 28.1 %collective-permute-start.2 = (bf16[2,8,2,64,128]{4,3,2,1,0:T(8,128)(2,1)}, bf16[2,8,2,64,128]{4,3,2,1,0:T(8,128)(2,1)S(1)}, u32[]{:S(2)}, u32[]{:S(2)}) collective-permute-start(bf16[2,8,2,64,128]{4,3,2,1,0:T(8,128)(2,1)} %get-tuple-element.32), channel_id=1, source_target_pairs={{0,24},{8,0},{16,8},{24,16},{1,25},{9,1},{17,9},{25,17},{2,26},{10... | collective-permute-start | bytes 1572872 | tf_op jit(solution)/shard_map/ppermute | solution.py:478
  30.6 26.7 %collective-permute-start.3 = (bf16[2,8,2,64,128]{4,3,2,1,0:T(8,128)(2,1)}, bf16[2,8,2,64,128]{4,3,2,1,0:T(8,128)(2,1)S(1)}, u32[]{:S(2)}, u32[]{:S(2)}) collective-permute-start(bf16[2,8,2,64,128]{4,3,2,1,0:T(8,128)(2,1)} %get-tuple-element.33), channel_id=1, source_target_pairs={{0,16},{8,24},{16,0},{24,8},{1,17},{9,25},{17,1},{25,9},{2,18},{10... | collective-permute-start | bytes 1572872 | tf_op jit(solution)/shard_map/ppermute | solution.py:478
  36.0 30.7 %collective-permute-start.4 = (bf16[2,8,2,64,128]{4,3,2,1,0:T(8,128)(2,1)}, bf16[2,8,2,64,128]{4,3,2,1,0:T(8,128)(2,1)S(1)}, u32[]{:S(2)}, u32[]{:S(2)}) collective-permute-start(bf16[2,8,2,64,128]{4,3,2,1,0:T(8,128)(2,1)} %get-tuple-element.34), channel_id=1, source_target_pairs={{0,8},{8,16},{16,24},{24,0},{1,9},{9,17},{17,25},{25,1},{2,10},{10... | collective-permute-start | bytes 1572872 | tf_op jit(solution)/shard_map/ppermute | solution.py:478
  48.2 43.6 %collective-permute-start.10 = (bf16[2,8,2,64,128]{4,3,2,1,0:T(8,128)(2,1)}, bf16[2,8,2,64,128]{4,3,2,1,0:T(8,128)(2,1)S(1)}, u32[]{:S(2)}, u32[]{:S(2)}) collective-permute-start(bf16[2,8,2,64,128]{4,3,2,1,0:T(8,128)(2,1)} %get-tuple-element.43.refs_4_.refs_3_), channel_id=1, source_target_pairs={{0,32},{32,64},{64,96},{96,128},{128,160},{160,192},{192,224},{224... | collective-permute-start | bytes 1572872 | tf_op jit(solution)/shard_map/ppermute | solution.py:478
  50.1 41.7 %collective-permute-start.11 = (bf16[2,8,2,64,128]{4,3,2,1,0:T(8,128)(2,1)}, bf16[2,8,2,64,128]{4,3,2,1,0:T(8,128)(2,1)S(1)}, u32[]{:S(2)}, u32[]{:S(2)}) collective-permute-start(bf16[2,8,2,64,128]{4,3,2,1,0:T(8,128)(2,1)} %get-tuple-element.44.refs_1_.refs_0_), channel_id=1, source_target_pairs={{0,224},{32,0},{64,32},{96,64},{128,96},{160,128},{192,160},{224,1... | collective-permute-start | bytes 1572872 | tf_op jit(solution)/shard_map/ppermute | solution.py:478
  69.3 29.2 %collective-permute-start.5 = (bf16[2,8,2,64,128]{4,3,2,1,0:T(8,128)(2,1)}, bf16[2,8,2,64,128]{4,3,2,1,0:T(8,128)(2,1)S(1)}, u32[]{:S(2)}, u32[]{:S(2)}) collective-permute-start(bf16[2,8,2,64,128]{4,3,2,1,0:T(8,128)(2,1)} %get-tuple-element.35.refs_3_.refs_4_), channel_id=1, source_target_pairs={{0,32},{32,64},{64,96},{96,128},{128,160},{160,192},{192,224},{224... | collective-permute-start | bytes 1572872 | tf_op jit(solution)/shard_map/ppermute | solution.py:478
  71.2 27.3 %collective-permute-start.6 = (bf16[2,8,2,64,128]{4,3,2,1,0:T(8,128)(2,1)}, bf16[2,8,2,64,128]{4,3,2,1,0:T(8,128)(2,1)S(1)}, u32[]{:S(2)}, u32[]{:S(2)}) collective-permute-start(bf16[2,8,2,64,128]{4,3,2,1,0:T(8,128)(2,1)} %get-tuple-element.36.refs_0_.refs_1_), channel_id=1, source_target_pairs={{0,224},{32,0},{64,32},{96,64},{128,96},{160,128},{192,160},{224,1... | collective-permute-start | bytes 1572872 | tf_op jit(solution)/shard_map/ppermute | solution.py:478
  105.9 16.0 %all-to-all-start = ((f32[8,48,128]{2,1,0:T(8,128)}), f32[8,48,128]{2,1,0:T(8,128)S(1)}, u32[]{:S(2)}, u32[]{:S(2)}) async-start(f32[8,48,128]{2,1,0:T(8,128)} %shard_map.71), calls=%async_computation | async-start | bytes 393216 | tf_op jit(solution)/shard_map/all_to_all | solution.py:510

commit v3 on v2

--- a/solution.py
+++ b/solution.py
@@ -415,10 +415,11 @@
         functools.partial(inner_kernel if inner else outer_kernel, tiles, not before, last),
         out_shape=outs,
         in_specs=[pl.BlockSpec(memory_space=pltpu.SMEM)]
-        + [vmem if not inner and u in (0, 5) else pl.BlockSpec(memory_space=pl.ANY) for u in range(len(units))]
+        + [vmem] * len(units)
         + [vmem] * len((*before, *extra)),
         out_specs=[vmem] * 2 if isinstance(outs, list) else vmem,
         scratch_shapes=scratch,
+        compiler_params=pltpu.CompilerParams(vmem_limit_bytes=24 << 20),
     )(tab, *units, *before, *extra)
 
 
@@ -463,9 +464,10 @@
     vmem = pl.BlockSpec(memory_space=pltpu.VMEM)
     return pl.pallas_call(
         arrange_kernel,
-        out_shape=[jax.ShapeDtypeStruct(p.shape, p.dtype) for p in pieces],
+        out_shape=[pltpu.VMEM(p.shape, p.dtype) for p in pieces],
         in_specs=[pl.BlockSpec(memory_space=pltpu.SMEM)] + [vmem] * 4,
         out_specs=[vmem] * 4,
+        compiler_params=pltpu.CompilerParams(vmem_limit_bytes=8 << 20),
     )(x, *pieces)
 
 

time: 125 us -> 120 us (0.960)
  Pallas kernels: 64.3 us -> 55.1 us
  local copies, waits for them, and re-layouts: 0 us -> 4.64 us
    pallas_call x4, Pallas kernels: 28.7 us -> 23.4 us  [coherence(): pl.pallas_call(functools.partial(inner_kernel if inner else outer_kernel,...]
    unnamed x0 -> x14, local copies, waits for them, and re-layouts: none -> 4.64 us
    pallas_call x2, Pallas kernels: 5.25 us -> 1.31 us  [arrange(): pl.pallas_call(arrange_kernel, out_shape=[pltpu.VMEM(p.shape, p.dtype) fo...]
  transfers between devices with their start and end apart: 13 -> 13, of which waited for: 6 -> 6; matrix products, arithmetic and copies ran while one was open for 0% -> 0% of each run, Pallas kernels for 37% -> 31%
where the time goes in v3:
time: 120 us; the launch traced here: 119 us
  Pallas kernels  55.1 us (46%)
  starting transfers between devices  30.7 us (26%)
  waiting for transfers between devices  28.5 us (24%)
  local copies, waits for them, and re-layouts  4.64 us (4%)
    ppermute x10, waiting for transfers between devices, shift(): return lax.ppermute(v, axis, [(i, (i + step) % size) for i in range(size)])  25.8 us
    pallas_call x4, Pallas kernels, coherence(): pl.pallas_call(functools.partial(inner_kernel if inner else outer_kernel,...  23.4 us
    ppermute x10, starting transfers between devices, shift(): return lax.ppermute(v, axis, [(i, (i + step) % size) for i in range(size)])  19.5 us
    pallas_call x2, Pallas kernels, resample(): pl.pallas_call(functools.partial(resample_kernel, tiles, needed, halo_in,...  18.1 us
    pallas_call x1, Pallas kernels, inverse(): pl.pallas_call(inverse_kernel, out_shape=jax.ShapeDtypeStruct((DATES, DAT...  8.38 us
    all_to_all x1, starting transfers between devices, per_device(): lax.all_to_all(outs, 'z', split_axis=0, concat_axis=0, tiled=True)  5.57 us
    unnamed x14, local copies, waits for them, and re-layouts  4.64 us
    ppermute x1, starting transfers between devices, per_device(): lax.ppermute(got[4], 'rng', [(i + 1, i) for i in range(size - 1)])  3.64 us
  transfers between devices with their start and end apart: 13, of which 6 were waited for; matrix products, arithmetic and copies ran while one was open for 0% of the time, Pallas kernels for 31%

profile of v3, /device:TPU:16, one launch (start us, length us, event | category | flops | bytes accessed | tf_op | source)
XLA Modules:
  0.0 119.0 jit_solution(8693103079901431298)
XLA Ops:
  0.0 9.2 %shard_map.64 = (bf16[2,8,2,64,128]{4,3,2,1,0:T(8,128)(2,1)}, bf16[2,8,2,64,128]{4,3,2,1,0:T(8,128)(2,1)}, bf16[2,8,2,64,128]{4,3,2,1,0:T(8,128)(2,1)}, bf16[2,8...) custom-call(s32[4,2,8]{2,1,0:T(2,128)} %bitcast.9, f32[8,8]{1,0:T(8,128)} %taps_ref.3, ...), custom_call_target="tpu_custom_call" | custom-call | tf_op jit(solution)/shard_map/pallas_call | solution.py:140
  9.3 2.8 %collective-permute-start.7 = (bf16[2,8,2,64,128]{4,3,2,1,0:T(8,128)(2,1)}, bf16[2,8,2,64,128]{4,3,2,1,0:T(8,128)(2,1)S(1)}, u32[]{:S(2)}, u32[]{:S(2)}) collective-permute-start(bf16[2,8,2,64,128]{4,3,2,1,0:T(8,128)(2,1)} %get-tuple-element.40), channel_id=1, source_target_pairs={{0,24},{8,0},{16,8},{24,16},{1,25},{9,1},{17,9},{25,17},{2,26},{10... | collective-permute-start | bytes 1572872 | tf_op jit(solution)/shard_map/ppermute | solution.py:480
  12.1 1.9 %collective-permute-start = (bf16[2,256,128]{2,1,0:T(8,128)(2,1)}, bf16[2,256,128]{2,1,0:T(8,128)(2,1)S(1)}, u32[]{:S(2)}, u32[]{:S(2)}) collective-permute-start(bf16[2,256,128]{2,1,0:T(8,128)(2,1)} %get-tuple-element.29), channel_id=1, source_target_pairs={{0,1},{1,2},{2,3},{3,4},{4,5},{5,6},{6,7},{8,9},{9,10},{10,11},{11... | collective-permute-start | bytes 393224 | tf_op jit(solution)/shard_map/ppermute | solution.py:496
  14.0 3.6 %collective-permute-start.1 = (bf16[2,256,128]{2,1,0:T(8,128)(2,1)}, bf16[2,256,128]{2,1,0:T(8,128)(2,1)S(1)}, u32[]{:S(2)}, u32[]{:S(2)}) collective-permute-start(bf16[2,256,128]{2,1,0:T(8,128)(2,1)} %get-tuple-element.30), channel_id=1, source_target_pairs={{1,0},{2,1},{3,2},{4,3},{5,4},{6,5},{7,6},{9,8},{10,9},{11,10},{12... | collective-permute-start | bytes 393224 | tf_op jit(solution)/shard_map/ppermute | solution.py:495
  20.5 8.8 %shard_map.65 = (bf16[2,8,2,64,128]{4,3,2,1,0:T(8,128)(2,1)}, bf16[2,8,2,64,128]{4,3,2,1,0:T(8,128)(2,1)}, bf16[2,8,2,64,128]{4,3,2,1,0:T(8,128)(2,1)}, bf16[2,8,2,64,128]{4,3,2,1,0:T(8,128)(2,1)}) custom-call(s32[4,2,8]{2,1,0:T(2,128)} %bitcast.10, f32[8,8]{1,0:T(8,128)} %taps_ref.3, s32[1]{0:T(128)} %bitcast.2.x_ref, bf16[8,2,256,512]{3,2,1,0:T(8,128)(2,1)} %refs_3_.3, ...), custom_call_target="tpu_custom_call" | custom-call | tf_op jit(solution)/shard_map/pallas_call | solution.py:140
  29.3 1.3 %collective-permute-start.2 = (bf16[2,8,2,64,128]{4,3,2,1,0:T(8,128)(2,1)}, bf16[2,8,2,64,128]{4,3,2,1,0:T(8,128)(2,1)S(1)}, u32[]{:S(2)}, u32[]{:S(2)}) collective-permute-start(bf16[2,8,2,64,128]{4,3,2,1,0:T(8,128)(2,1)} %get-tuple-element.32), channel_id=1, source_target_pairs={{0,24},{8,0},{16,8},{24,16},{1,25},{9,1},{17,9},{25,17},{2,26},{10... | collective-permute-start | bytes 1572872 | tf_op jit(solution)/shard_map/ppermute | solution.py:480
  30.6 1.5 %collective-permute-start.3 = (bf16[2,8,2,64,128]{4,3,2,1,0:T(8,128)(2,1)}, bf16[2,8,2,64,128]{4,3,2,1,0:T(8,128)(2,1)S(1)}, u32[]{:S(2)}, u32[]{:S(2)}) collective-permute-start(bf16[2,8,2,64,128]{4,3,2,1,0:T(8,128)(2,1)} %get-tuple-element.33), channel_id=1, source_target_pairs={{0,16},{8,24},{16,0},{24,8},{1,17},{9,25},{17,1},{25,9},{2,18},{10... | collective-permute-start | bytes 1572872 | tf_op jit(solution)/shard_map/ppermute | solution.py:480
  32.1 3.8 %collective-permute-done.7.refs_1_ = bf16[2,8,2,64,128]{4,3,2,1,0:T(8,128)(2,1)S(1)} collective-permute-done((bf16[2,8,2,64,128]{4,3,2,1,0:T(8,128)(2,1)}, bf16[2,8,2,64,128]{4,3,2,1,0:T(8,128)(2,1)S(1)}, u32[]{:S(2)}, u32[]{:S(2)}) %collective-permute-start.7) | collective-permute-done | bytes 524320 | tf_op jit(solution)/shard_map/ppermute | solution.py:480
  35.9 9.6 %collective-permute-done.9.refs_3_ = bf16[2,8,2,64,128]{4,3,2,1,0:T(8,128)(2,1)S(1)} collective-permute-done((bf16[2,8,2,64,128]{4,3,2,1,0:T(8,128)(2,1)}, bf16[2,8,2,64,128]{4,3,2,1,0:T(8,128)(2,1)S(1)}, u32[]{:S(2)}, u32[]{:S(2)}) %collective-permute-start.9) | collective-permute-done | bytes 524320 | tf_op jit(solution)/shard_map/ppermute | solution.py:480
  48.5 1.9 %collective-permute-start.10 = (bf16[2,8,2,64,128]{4,3,2,1,0:T(8,128)(2,1)}, bf16[2,8,2,64,128]{4,3,2,1,0:T(8,128)(2,1)}, u32[]{:S(2)}, u32[]{:S(2)}) collective-permute-start(bf16[2,8,2,64,128]{4,3,2,1,0:T(8,128)(2,1)} %get-tuple-element.43.refs_4_.refs_3_), channel_id=1, source_target_pairs={{0,32},{32,64},{64,96},{96,128},{128,160},{160,192},{192,224},{224... | collective-permute-start | bytes 1572872 | tf_op jit(solution)/shard_map/ppermute | solution.py:480
  50.4 3.9 %collective-permute-start.11 = (bf16[2,8,2,64,128]{4,3,2,1,0:T(8,128)(2,1)S(1)}, bf16[2,8,2,64,128]{4,3,2,1,0:T(8,128)(2,1)}, u32[]{:S(2)}, u32[]{:S(2)}) collective-permute-start(bf16[2,8,2,64,128]{4,3,2,1,0:T(8,128)(2,1)S(1)} %get-tuple-element.44.refs_1_.refs_0_), channel_id=1, source_target_pairs={{0,224},{32,0},{64,32},{96,64},{128,96},{160,128},{192,160},{224,1... | collective-permute-start | bytes 1572872 | tf_op jit(solution)/shard_map/ppermute | solution.py:480
  54.4 3.0 %collective-permute-done.2.refs_1_ = bf16[2,8,2,64,128]{4,3,2,1,0:T(8,128)(2,1)S(1)} collective-permute-done((bf16[2,8,2,64,128]{4,3,2,1,0:T(8,128)(2,1)}, bf16[2,8,2,64,128]{4,3,2,1,0:T(8,128)(2,1)S(1)}, u32[]{:S(2)}, u32[]{:S(2)}) %collective-permute-start.2) | collective-permute-done | bytes 524320 | tf_op jit(solution)/shard_map/ppermute | solution.py:480
  57.3 9.3 %collective-permute-done.4.refs_3_ = bf16[2,8,2,64,128]{4,3,2,1,0:T(8,128)(2,1)S(1)} collective-permute-done((bf16[2,8,2,64,128]{4,3,2,1,0:T(8,128)(2,1)}, bf16[2,8,2,64,128]{4,3,2,1,0:T(8,128)(2,1)S(1)}, u32[]{:S(2)}, u32[]{:S(2)}) %collective-permute-start.4) | collective-permute-done | bytes 524320 | tf_op jit(solution)/shard_map/ppermute | solution.py:480
  67.9 2.0 %collective-permute-start.5 = (bf16[2,8,2,64,128]{4,3,2,1,0:T(8,128)(2,1)S(1)}, bf16[2,8,2,64,128]{4,3,2,1,0:T(8,128)(2,1)}, u32[]{:S(2)}, u32[]{:S(2)}) collective-permute-start(bf16[2,8,2,64,128]{4,3,2,1,0:T(8,128)(2,1)S(1)} %get-tuple-element.35.refs_3_.refs_4_), channel_id=1, source_target_pairs={{0,32},{32,64},{64,96},{96,128},{128,160},{160,192},{192,224},{224... | collective-permute-start | bytes 1572872 | tf_op jit(solution)/shard_map/ppermute | solution.py:480
  70.0 4.2 %collective-permute-start.6 = (bf16[2,8,2,64,128]{4,3,2,1,0:T(8,128)(2,1)S(1)}, bf16[2,8,2,64,128]{4,3,2,1,0:T(8,128)(2,1)}, u32[]{:S(2)}, u32[]{:S(2)}) collective-permute-start(bf16[2,8,2,64,128]{4,3,2,1,0:T(8,128)(2,1)S(1)} %get-tuple-element.36.refs_0_.refs_1_), channel_id=1, source_target_pairs={{0,224},{32,0},{64,32},{96,64},{128,96},{160,128},{192,160},{224,1... | collective-permute-start | bytes 1572872 | tf_op jit(solution)/shard_map/ppermute | solution.py:480
  74.2 2.0 %table.1.tab_ref = s32[32,128]{1,0:T(8,128)} custom-call(s32[1]{0:T(128)} %bitcast.1.first_ref, s32[2,1024]{1,0:T(2,128)} %bitcast.7), custom_call_target="tpu_custom_call" | custom-call | tf_op jit(solution)/shard_map/table/pallas_call | solution.py:168
  77.9 5.6 %shard_map.69 = (f32[512,128]{1,0:T(8,128)S(1)}, f32[256,128]{1,0:T(8,128)S(1)}) custom-call(s32[32,128]{1,0:T(8,128)S(1)} %copy-done.6, bf16[2,8,2,64,128]{4,3,2,1,0:T(8,128)(2,1)S(1)} %get-tuple-element.44.refs_1_.refs_0_, bf16[2,8,2,64,128]{4,3,2,1,0:T(8,128)(2,1)S(1)} %get-tuple-element.45.refs_2_.refs_1_, bf16[2,8,2,64,128]{4,3,2,1,0:T(8,128)(2,1)S(1)} %copy-done.1, ...), custom_call_target="tpu_custom_call" | custom-call | tf_op jit(solution)/shard_map/pallas_call | solution.py:414
  83.5 5.7 %shard_map.70 = (f32[384,128]{1,0:T(8,128)S(1)}, f32[256,128]{1,0:T(8,128)S(1)}) custom-call(s32[32,128]{1,0:T(8,128)S(1)} %copy-done.6, bf16[2,8,2,64,128]{4,3,2,1,0:T(8,128)(2,1)S(1)} %get-tuple-element.36.refs_0_.refs_1_, bf16[2,8,2,64,128]{4,3,2,1,0:T(8,128)(2,1)S(1)} %get-tuple-element.37.refs_1_.refs_2_, ...), custom_call_target="tpu_custom_call" | custom-call | tf_op jit(solution)/shard_map/pallas_call | solution.py:414
  89.3 5.6 %shard_map.68 = (f32[512,128]{1,0:T(8,128)S(1)}, f32[128,128]{1,0:T(8,128)S(1)}) custom-call(s32[32,128]{1,0:T(8,128)S(1)} %copy-done.6, bf16[2,8,2,64,128]{4,3,2,1,0:T(8,128)(2,1)} %collective-permute-done.10.refs_0_, bf16[2,8,2,64,128]{4,3,2,1,0:T(8,128)(2,1)S(1)} %get-tuple-element.44.refs_1_.refs_0_, ...), custom_call_target="tpu_custom_call" | custom-call | tf_op jit(solution)/shard_map/pallas_call | solution.py:414
  94.9 6.5 %shard_map.71 = f32[8,48,128]{2,1,0:T(8,128)} custom-call(s32[32,128]{1,0:T(8,128)S(1)} %copy-done.6, bf16[2,8,2,64,128]{4,3,2,1,0:T(8,128)(2,1)} %collective-permute-done.5.refs_0_, bf16[2,8,2,64,128]{4,3,2,1,0:T(8,128)(2,1)S(1)} %get-tuple-element.36.refs_0_.refs_1_, bf16[2,8,2,64,128]{4,3,2,1,0:T(8,128)(2,1)S(1)} %get-tuple-element.37.refs_1_.refs_2_, ...), custom_call_target="tpu_custom_call" | custom-call | tf_op jit(solution)/shard_map/pallas_call | solution.py:414
  101.4 5.6 %all-to-all-start = ((f32[8,48,128]{2,1,0:T(8,128)}), f32[8,48,128]{2,1,0:T(8,128)S(1)}, u32[]{:S(2)}, u32[]{:S(2)}) async-start(f32[8,48,128]{2,1,0:T(8,128)} %shard_map.71), calls=%async_computation | async-start | bytes 393216 | tf_op jit(solution)/shard_map/all_to_all | solution.py:512
  107.0 8.4 %inverse.1.inv_ref = f32[256,256]{1,0:T(8,128)} custom-call(s32[2,1024]{1,0:T(2,128)} %bitcast.8), custom_call_target="tpu_custom_call" | custom-call | tf_op jit(solution)/shard_map/inverse/pallas_call | solution.py:213
  115.3 1.7 %all-to-all-done.got_ref = f32[8,48,128]{2,1,0:T(8,128)S(1)} async-done(((f32[8,48,128]{2,1,0:T(8,128)}), f32[8,48,128]{2,1,0:T(8,128)S(1)}, u32[]{:S(2)}, u32[]{:S(2)}) %all-to-all-start) | async-done | bytes 196640 | tf_op jit(solution)/shard_map/all_to_all | solution.py:512
  117.0 1.9 %solve.1 = f32[128,256]{1,0:T(8,128)} custom-call(f32[256,256]{1,0:T(8,128)} %inverse.1.inv_ref, f32[8,48,128]{2,1,0:T(8,128)S(1)} %all-to-all-done.got_ref), custom_call_target="tpu_custom_call" | custom-call | tf_op jit(solution)/shard_map/solve/pallas_call | solution.py:443
  (27 shorter events, 8.8 us)
Async XLA Ops:
  9.3 26.7 %collective-permute-start.7 = (bf16[2,8,2,64,128]{4,3,2,1,0:T(8,128)(2,1)}, bf16[2,8,2,64,128]{4,3,2,1,0:T(8,128)(2,1)S(1)}, u32[]{:S(2)}, u32[]{:S(2)}) collective-permute-start(bf16[2,8,2,64,128]{4,3,2,1,0:T(8,128)(2,1)} %get-tuple-element.40), channel_id=1, source_target_pairs={{0,24},{8,0},{16,8},{24,16},{1,25},{9,1},{17,9},{25,17},{2,26},{10... | collective-permute-start | bytes 1572872 | tf_op jit(solution)/shard_map/ppermute | solution.py:480
  12.1 7.4 %collective-permute-start = (bf16[2,256,128]{2,1,0:T(8,128)(2,1)}, bf16[2,256,128]{2,1,0:T(8,128)(2,1)S(1)}, u32[]{:S(2)}, u32[]{:S(2)}) collective-permute-start(bf16[2,256,128]{2,1,0:T(8,128)(2,1)} %get-tuple-element.29), channel_id=1, source_target_pairs={{0,1},{1,2},{2,3},{3,4},{4,5},{5,6},{6,7},{8,9},{9,10},{10,11},{11... | collective-permute-start | bytes 393224 | tf_op jit(solution)/shard_map/ppermute | solution.py:496
  14.0 6.5 %collective-permute-start.1 = (bf16[2,256,128]{2,1,0:T(8,128)(2,1)}, bf16[2,256,128]{2,1,0:T(8,128)(2,1)S(1)}, u32[]{:S(2)}, u32[]{:S(2)}) collective-permute-start(bf16[2,256,128]{2,1,0:T(8,128)(2,1)} %get-tuple-element.30), channel_id=1, source_target_pairs={{1,0},{2,1},{3,2},{4,3},{5,4},{6,5},{7,6},{9,8},{10,9},{11,10},{12... | collective-permute-start | bytes 393224 | tf_op jit(solution)/shard_map/ppermute | solution.py:495
  17.6 18.3 %collective-permute-start.8 = (bf16[2,8,2,64,128]{4,3,2,1,0:T(8,128)(2,1)}, bf16[2,8,2,64,128]{4,3,2,1,0:T(8,128)(2,1)S(1)}, u32[]{:S(2)}, u32[]{:S(2)}) collective-permute-start(bf16[2,8,2,64,128]{4,3,2,1,0:T(8,128)(2,1)} %get-tuple-element.41), channel_id=1, source_target_pairs={{0,16},{8,24},{16,0},{24,8},{1,17},{9,25},{17,1},{25,9},{2,18},{10... | collective-permute-start | bytes 1572872 | tf_op jit(solution)/shard_map/ppermute | solution.py:480
  18.5 27.8 %copy-start.2 = (bf16[2,8,2,64,128]{4,3,2,1,0:T(8,128)(2,1)S(1)}, bf16[2,8,2,64,128]{4,3,2,1,0:T(8,128)(2,1)}, u32[]{:S(2)}) copy-start(bf16[2,8,2,64,128]{4,3,2,1,0:T(8,128)(2,1)} %get-tuple-element.39.refs_0_) | copy-start | bytes 1572868
  18.5 27.0 %collective-permute-start.9 = (bf16[2,8,2,64,128]{4,3,2,1,0:T(8,128)(2,1)}, bf16[2,8,2,64,128]{4,3,2,1,0:T(8,128)(2,1)S(1)}, u32[]{:S(2)}, u32[]{:S(2)}) collective-permute-start(bf16[2,8,2,64,128]{4,3,2,1,0:T(8,128)(2,1)} %get-tuple-element.42), channel_id=1, source_target_pairs={{0,8},{8,16},{16,24},{24,0},{1,9},{9,17},{17,25},{25,1},{2,10},{10... | collective-permute-start | bytes 1572872 | tf_op jit(solution)/shard_map/ppermute | solution.py:480
  29.3 28.0 %collective-permute-start.2 = (bf16[2,8,2,64,128]{4,3,2,1,0:T(8,128)(2,1)}, bf16[2,8,2,64,128]{4,3,2,1,0:T(8,128)(2,1)S(1)}, u32[]{:S(2)}, u32[]{:S(2)}) collective-permute-start(bf16[2,8,2,64,128]{4,3,2,1,0:T(8,128)(2,1)} %get-tuple-element.32), channel_id=1, source_target_pairs={{0,24},{8,0},{16,8},{24,16},{1,25},{9,1},{17,9},{25,17},{2,26},{10... | collective-permute-start | bytes 1572872 | tf_op jit(solution)/shard_map/ppermute | solution.py:480
  30.6 26.7 %collective-permute-start.3 = (bf16[2,8,2,64,128]{4,3,2,1,0:T(8,128)(2,1)}, bf16[2,8,2,64,128]{4,3,2,1,0:T(8,128)(2,1)S(1)}, u32[]{:S(2)}, u32[]{:S(2)}) collective-permute-start(bf16[2,8,2,64,128]{4,3,2,1,0:T(8,128)(2,1)} %get-tuple-element.33), channel_id=1, source_target_pairs={{0,16},{8,24},{16,0},{24,8},{1,17},{9,25},{17,1},{25,9},{2,18},{10... | collective-permute-start | bytes 1572872 | tf_op jit(solution)/shard_map/ppermute | solution.py:480
  35.9 30.7 %collective-permute-start.4 = (bf16[2,8,2,64,128]{4,3,2,1,0:T(8,128)(2,1)}, bf16[2,8,2,64,128]{4,3,2,1,0:T(8,128)(2,1)S(1)}, u32[]{:S(2)}, u32[]{:S(2)}) collective-permute-start(bf16[2,8,2,64,128]{4,3,2,1,0:T(8,128)(2,1)} %get-tuple-element.34), channel_id=1, source_target_pairs={{0,8},{8,16},{16,24},{24,0},{1,9},{9,17},{17,25},{25,1},{2,10},{10... | collective-permute-start | bytes 1572872 | tf_op jit(solution)/shard_map/ppermute | solution.py:480
  45.6 0.8 copy-start.4
  46.4 1.0 copy-start.5
  48.5 21.5 %copy-start = (bf16[2,8,2,64,128]{4,3,2,1,0:T(8,128)(2,1)}, bf16[2,8,2,64,128]{4,3,2,1,0:T(8,128)(2,1)S(1)}, u32[]{:S(2)}) copy-start(bf16[2,8,2,64,128]{4,3,2,1,0:T(8,128)(2,1)S(1)} %get-tuple-element.46.refs_3_.refs_2_) | copy-start | bytes 1572868
  48.5 40.8 %collective-permute-start.10 = (bf16[2,8,2,64,128]{4,3,2,1,0:T(8,128)(2,1)}, bf16[2,8,2,64,128]{4,3,2,1,0:T(8,128)(2,1)}, u32[]{:S(2)}, u32[]{:S(2)}) collective-permute-start(bf16[2,8,2,64,128]{4,3,2,1,0:T(8,128)(2,1)} %get-tuple-element.43.refs_4_.refs_3_), channel_id=1, source_target_pairs={{0,32},{32,64},{64,96},{96,128},{128,160},{160,192},{192,224},{224... | collective-permute-start | bytes 1572872 | tf_op jit(solution)/shard_map/ppermute | solution.py:480
  50.4 38.8 %collective-permute-start.11 = (bf16[2,8,2,64,128]{4,3,2,1,0:T(8,128)(2,1)S(1)}, bf16[2,8,2,64,128]{4,3,2,1,0:T(8,128)(2,1)}, u32[]{:S(2)}, u32[]{:S(2)}) collective-permute-start(bf16[2,8,2,64,128]{4,3,2,1,0:T(8,128)(2,1)S(1)} %get-tuple-element.44.refs_1_.refs_0_), channel_id=1, source_target_pairs={{0,224},{32,0},{64,32},{96,64},{128,96},{160,128},{192,160},{224,1... | collective-permute-start | bytes 1572872 | tf_op jit(solution)/shard_map/ppermute | solution.py:480
  66.6 1.0 copy-start.3
  67.9 26.9 %collective-permute-start.5 = (bf16[2,8,2,64,128]{4,3,2,1,0:T(8,128)(2,1)S(1)}, bf16[2,8,2,64,128]{4,3,2,1,0:T(8,128)(2,1)}, u32[]{:S(2)}, u32[]{:S(2)}) collective-permute-start(bf16[2,8,2,64,128]{4,3,2,1,0:T(8,128)(2,1)S(1)} %get-tuple-element.35.refs_3_.refs_4_), channel_id=1, source_target_pairs={{0,32},{32,64},{64,96},{96,128},{128,160},{160,192},{192,224},{224... | collective-permute-start | bytes 1572872 | tf_op jit(solution)/shard_map/ppermute | solution.py:480
  70.0 24.9 %collective-permute-start.6 = (bf16[2,8,2,64,128]{4,3,2,1,0:T(8,128)(2,1)S(1)}, bf16[2,8,2,64,128]{4,3,2,1,0:T(8,128)(2,1)}, u32[]{:S(2)}, u32[]{:S(2)}) collective-permute-start(bf16[2,8,2,64,128]{4,3,2,1,0:T(8,128)(2,1)S(1)} %get-tuple-element.36.refs_0_.refs_1_), channel_id=1, source_target_pairs={{0,224},{32,0},{64,32},{96,64},{128,96},{160,128},{192,160},{224,1... | collective-permute-start | bytes 1572872 | tf_op jit(solution)/shard_map/ppermute | solution.py:480
  76.1 1.0 copy-start.1
  77.2 0.7 copy-start.6
  101.4 15.7 %all-to-all-start = ((f32[8,48,128]{2,1,0:T(8,128)}), f32[8,48,128]{2,1,0:T(8,128)S(1)}, u32[]{:S(2)}, u32[]{:S(2)}) async-start(f32[8,48,128]{2,1,0:T(8,128)} %shard_map.71), calls=%async_computation | async-start | bytes 393216 | tf_op jit(solution)/shard_map/all_to_all | solution.py:512
